TPU v7x, 256 devices: a whole 4x4x8 slice. The times are simulated.
256 devices in a mesh: cand: 32 (over y_lo, z, core), img: 8 (over y_hi, x).
Axes of the slice: x: 4, y: 4 (y_hi: 2, y_lo: 2; y = y_hi * 2 + y_lo), z: 8, core: 2. Of those that a mesh axis runs over, the one named last changes fastest.
Arguments:
- first_maps: float32 [8, 256, 344], P('img', 'cand'), may hold values from -6 to 6
- layer_of: int32 [32], P('cand'), may hold values from 0 to 1, as said below
- expand_half: int32 [32], P('cand'), may hold values from 1 to 2
- radius: int32 [32], P('cand'), may hold values from 1 to 2
- teach_up: bfloat16 [2, 344, 2064], replicated, may hold values from -0.3125 to 0.3125
- teach_dw: float32 [2, 25, 2064], replicated, may hold values from -1.25 to 1.25
- teach_down: bfloat16 [2, 344, 2064], replicated, may hold values from -0.125 to 0.125
- cand_up: bfloat16 [32, 344, 2064], P('cand'), may hold values from -0.3125 to 0.3125
- cand_dw: float32 [32, 25, 2064], P('cand'), may hold values from -1.25 to 1.25
- cand_down: bfloat16 [32, 344, 2064], P('cand'), may hold values from -0.125 to 0.125
Outputs:
- grad_up: float32 [32, 344, 2064], P('cand', None, 'img')
- grad_dw: float32 [32, 25, 2064], P('cand', None, 'img')
- grad_down: float32 [32, 344, 2064], P('cand', None, 'img')
Inputs may be any that keep to these rules, and one draw needn't show every extreme that they name: `layer_of`: both layers have at least one candidate.
All inputs are finite; a program needn't handle non-finite values.
Results may differ from a plain program's by a relative error of at most 0.014.
Values may be sent and summed in bfloat16 or wider, within the bound.
A program may use at most 192 MiB of HBM per device.

v0:
```python
import jax
import jax.numpy as jnp
from jax import lax
from jax.sharding import PartitionSpec as P

HID = 2064
H = 16


def spread(block, axis, source):
    block = jnp.where(lax.axis_index(axis) == source, block, jnp.zeros_like(block))
    return lax.psum(block, axis)


def apply_block(map_in, w_up, w_dw, w_down, unit_mask, tap_mask):
    batch_size = map_in.shape[0]
    flat_rows = map_in.reshape(-1, map_in.shape[2]).astype(jnp.bfloat16)
    preact = jnp.dot(flat_rows, w_up, preferred_element_type=jnp.float32)
    expanded = jax.nn.silu(preact) * unit_mask
    grid_maps = expanded.reshape(batch_size, H, H, expanded.shape[1])
    padded = jnp.pad(grid_maps, ((0, 0), (2, 2), (2, 2), (0, 0)))
    tap_weights = w_dw * tap_mask[:, None]
    accumulated = jnp.zeros_like(grid_maps)
    for tap_row in range(5):
        for tap_col in range(5):
            accumulated = (
                accumulated
                + tap_weights[tap_row * 5 + tap_col]
                * padded[:, tap_row : tap_row + H, tap_col : tap_col + H, :]
            )
    activated = jax.nn.silu(accumulated).reshape(-1, grid_maps.shape[3]).astype(jnp.bfloat16)
    branch = lax.dot_general(
        activated, w_down, (((1,), (1,)), ((), ())), preferred_element_type=jnp.float32
    )
    return map_in + branch.reshape(map_in.shape)


def make_masks(half_count, kernel_radius):
    unit_index = lax.broadcasted_iota(jnp.int32, (HID,), 0)
    unit_mask = (unit_index < half_count * (HID // 2)).astype(jnp.float32)
    tap_index = lax.broadcasted_iota(jnp.int32, (25,), 0)
    shift_row = tap_index // 5 - 2
    shift_col = tap_index % 5 - 2
    tap_mask = (jnp.maximum(jnp.abs(shift_row), jnp.abs(shift_col)) <= kernel_radius).astype(
        jnp.float32
    )
    return (unit_mask, tap_mask)


def candidate_grads(inputs, target, w_up, w_dw, w_down, unit_mask, tap_mask, images):

    def squared_loss(up_wide, depth_weights, down_wide):
        result = apply_block(
            inputs,
            up_wide.astype(jnp.bfloat16),
            depth_weights,
            down_wide.astype(jnp.bfloat16),
            unit_mask,
            tap_mask,
        )
        error_map = result - target
        return 0.5 * jnp.sum(error_map * error_map) / images

    return jax.grad(squared_loss, argnums=(0, 1, 2))(
        w_up.astype(jnp.float32), w_dw, w_down.astype(jnp.float32)
    )


def body(
    first_maps,
    layer_of,
    expand_half,
    radius,
    teach_up,
    teach_dw,
    teach_down,
    cand_up,
    cand_dw,
    cand_down,
):
    cand_index = lax.axis_index("cand")
    layer_here = layer_of[0]
    maps_zero = lax.all_gather(first_maps, "cand", axis=1, tiled=True)
    full_units = jnp.ones((HID,), jnp.float32)
    all_taps = jnp.ones((25,), jnp.float32)

    def teacher(map_in, depth_level):
        return apply_block(
            map_in,
            teach_up[depth_level],
            teach_dw[depth_level],
            teach_down[depth_level],
            full_units,
            all_taps,
        )

    beyond = jnp.int32(lax.axis_size("cand"))
    owner_ranks = lax.pmin(
        (
            jnp.where(layer_here == 0, cand_index, beyond),
            jnp.where(layer_here == 1, cand_index, beyond),
        ),
        "cand",
    )

    def announce(map_in, depth_level, owner_rank):
        produced = lax.cond(
            cand_index == owner_rank,
            lambda: teacher(map_in, depth_level),
            lambda: jnp.zeros_like(map_in),
        )
        return spread(produced.astype(jnp.bfloat16), "cand", owner_rank).astype(produced.dtype)

    maps_one = announce(maps_zero, 0, owner_ranks[0])
    maps_two = announce(maps_one, 1, owner_ranks[1])
    inputs = jnp.where(layer_here == 0, maps_zero, maps_one)
    target = jnp.where(layer_here == 0, maps_one, maps_two)
    unit_mask, tap_mask = make_masks(expand_half[0], radius[0])
    images = maps_zero.shape[0] * lax.axis_size("img")
    gradients = candidate_grads(
        inputs, target, cand_up[0], cand_dw[0], cand_down[0], unit_mask, tap_mask, images
    )
    summed = (
        lax.psum_scatter(
            gradients[0][None].astype(jnp.bfloat16), "img", scatter_dimension=2, tiled=True
        ).astype(jnp.float32),
        lax.psum_scatter(
            gradients[1][None].astype(jnp.bfloat16), "img", scatter_dimension=2, tiled=True
        ).astype(jnp.float32),
        lax.psum_scatter(
            gradients[2][None].astype(jnp.bfloat16), "img", scatter_dimension=2, tiled=True
        ).astype(jnp.float32),
    )
    return (summed[0], summed[1], summed[2])


def solution(mesh):
    placed = (
        P("img", "cand", None),
        P("cand"),
        P("cand"),
        P("cand"),
        P(),
        P(),
        P(),
        P("cand", None, None),
        P("cand", None, None),
        P("cand", None, None),
    )
    return jax.shard_map(
        body,
        mesh=mesh,
        in_specs=placed,
        out_specs=(P("cand", None, "img"), P("cand", None, "img"), P("cand", None, "img")),
        check_vma=False,
    )
```

profile of v0, /device:TPU:1, one launch (start us, length us, event | category | flops | bytes accessed | tf_op | source)
XLA Modules:
  0.0 738.8 jit_solution(10471688653235527905)
XLA Ops:
  7.2 0.0 copy-start
  7.2 0.0 all-reduce.62.cloned.1.call-start
  8.0 17.8 %all-reduce.56 = (s32[]{:T(128)}, s32[]{:T(128)}) all-reduce(s32[]{:T(128)S(6)} %select_n.53, s32[]{:T(128)S(6)} %select_n.59), channel_id=1, replica_groups=mesh['cand'=32,'img'=8] {'cand'}, use_global_device_ids=true, to_apply=%region_0.1 | all-reduce | flops 2 | bytes 16 | tf_op jit(solution)/shard_map/pmin | solution.py:98
  26.5 0.7 copy.30
  27.2 35.9 %all_gather.3 = f32[1,256,344]{2,0,1:T(1,128)S(1)} all-gather(f32[1,8,344]{2,0,1:T(1,128)S(1)} %copy.30), channel_id=1, replica_groups=mesh['cand'=32,'img'=8] {'cand'}, dimensions={1}, use_global_device_ids=true | all-gather | bytes 363264 | tf_op jit(solution)/shard_map/all_gather | solution.py:83
  63.1 0.7 broadcast_select_fusion.1
  63.8 0.0 all-reduce.62.cloned.1.call-update
  63.9 0.0 all-reduce.64.cloned.1.call-start
  65.2 0.0 copy-done.5
  65.2 0.0 copy-start.46
  65.2 0.1 bitcast_multiply_fusion
  65.3 0.7 slice_reduce_fusion.73
  66.1 0.0 copy-done.46
  66.1 0.4 copy.33
  66.5 0.0 copy-start.4
  67.0 1.0 slice_reduce_fusion.74
  68.1 0.0 copy-start.18
  68.1 0.0 copy-start.20
  68.1 0.0 copy-start.22
  68.1 0.0 copy-start.24
  68.1 0.0 copy-start.26
  68.1 0.0 copy-start.28
  68.2 0.0 copy-start.30
  68.2 0.0 copy-start.32
  68.2 0.0 copy-start.34
  68.2 238.7 %all-reduce.62.cloned.1.call-done = bf16[1,256,344]{1,2,0:T(8,128)(2,1)} async-done(((bf16[1,256,344]{1,2,0:T(8,128)(2,1)}), bf16[1,256,344]{1,2,0:T(8,128)(2,1)}) %all-reduce.62.cloned.1.call-update) | async-done | bytes 176144 | tf_op jit(solution)/shard_map/psum | solution.py:12
  306.9 1.0 fusion.181
  307.9 0.0 copy-start.6
  307.9 0.0 copy-done.4
  307.9 0.0 copy-done
  307.9 3.0 multiply_multiply_fusion
  310.9 0.0 copy-done.44
  310.9 0.0 copy-done.6
  310.9 2.0 copy.34
  313.0 0.2 conditional.3
  313.2 0.7 broadcast_select_fusion
  313.9 0.0 all-reduce.64.cloned.1.call-update
  313.9 0.0 all-reduce.66.cloned.1.call-start
  314.1 9.7 %multiply_convert_fusion.2 = (bf16[1,16,16,2064]{3,2,1,0:T(8,128)(2,1)S(1)}, f32[1,16,16,2064]{3,2,1,0:T(8,128)}) fusion(f32[2064]{0:T(1024)S(1)} %get-tuple-element.143, f32[2064]{0:T(1024)S(1)} %get-tuple-element.144, f32[2064]{0:T(1024)S(1)} %get-tuple-element.145, f32[2064]{0:T(1024)S(1)} %get-tuple-element.146, f32[2064]{0:T(1024)S(1)} %get-tuple-element.147, ...), kind=kLoop, calls=%fused_computation.286 | loop fusion | flops 28532736 | bytes 5490240 | tf_op jit(solution)/shard_map/jvp()/convert_element_type | solution.py:31
  323.8 232.4 %all-reduce.64.cloned.1.call-done = bf16[1,256,344]{1,2,0:T(8,128)(2,1)} async-done(((bf16[1,256,344]{1,2,0:T(8,128)(2,1)}), bf16[1,256,344]{1,2,0:T(8,128)(2,1)}) %all-reduce.64.cloned.1.call-update) | async-done | bytes 176144 | tf_op jit(solution)/shard_map/psum | solution.py:12
  556.2 2.2 fusion.165
  558.5 2.2 fusion.134
  560.7 3.0 copy.36
  563.7 4.5 multiply_reduce_fusion.23
  568.3 0.0 copy-start.36
  568.4 6.6 multiply_reduce_fusion.24
  575.3 12.9 %broadcast_multiply_fusion.24 = (f32[1,16,16,2064]{3,2,1,0:T(8,128)}, f32[1,16,16,2064]{3,2,1,0:T(8,128)}, f32[1,16,16,2064]{3,2,1,0:T(8,128)}, f32[1,16,16,2064...) fusion(f32[1,16,16,2064]{3,2,1,0:T(8,128)S(1)} %get-tuple-eleme, ...), kind=kLoop, calls=%fused_computation.331 | loop fusion | flops 9510912 | bytes 40305792 | tf_op jit(solution)/shard_map/transpose(jvp())/mul | solution.py:28
  588.2 5.5 broadcast_multiply_fusion
  593.8 1.8 fusion.136
  595.9 0.4 multiply_convert_fusion.3
  596.3 0.8 convert_element_type.135
  597.1 16.1 %pad_add_fusion = f32[1,20,20,2064]{3,2,1,0:T(8,128)S(1)} fusion(f32[1,16,16,2064]{3,2,1,0:T(8,128)} %get-tuple-element.183, f32[1,16,16,2064]{3,2,1,0:T(8,128)} %get-tuple-element.184, f32[1,16,16,2064]{3,2,1,0:T(8,128)} %get-tuple-element.185, f32[1,16,16,2064]{3,2,1,0:T(8,128)} %get-tuple-element.186, f32[1,16,16,2064]{3,2,1,0:T(8,128)} %get-tuple-element.187, ...), kind=kLoop, calls=%fused_computation.244 | loop fusion | flops 14860800 | bytes 43459584 | tf_op jit(solution)/shard_map/transpose(jvp())/add_any | solution.py:29
  613.3 7.1 pad_add_fusion.1
  620.4 2.0 copy.37
  622.4 3.9 fusion.135
  626.3 0.0 all-reduce.66.cloned.1.call-update
  626.3 0.0 copy-start.1
  626.3 0.6 copy-done.50
  627.0 0.6 dynamic-slice
  628.2 98.7 %all-reduce.66.cloned.1.call-done = (bf16[1,344,2064]{2,1,0:T(8,128)(2,1)}, bf16[1,25,2064]{2,0,1:T(2,128)(2,1)}, bf16[1,344,2064]{2,1,0:T(8,128)(2,1)}) async-done(((bf16[1,344,2064]{2,1,0:T(8,128)(2,1)}, bf16[1,25,2064]{2,0,1:T(2,128)(2,1)}, bf16[1,344,2064]{2,1,0:T(8,128)(2,1)}), (bf16[1,344,2064]{2,1,0:T(8,128)(2,1)}, bf16[1,25,2064]{2,0,1:T(2,128)(2,1)}, ...) | async-done | bytes 2943280
  726.9 1.3 dynamic-slice_convert_fusion
  728.3 1.2 copy.38
  729.5 1.2 copy.39
  730.7 1.6 dynamic-slice_convert_fusion.2
  (106 shorter events, 0.4 us)
Async XLA Ops:
  7.2 300.7 %copy-start = (bf16[1,344,2064]{2,1,0:T(8,128)(2,1)S(1)}, bf16[1,344,2064]{2,1,0:T(8,128)(2,1)}, u32[]{:S(2)}) copy-start(bf16[1,344,2064]{2,1,0:T(8,128)(2,1)} %param.21) | copy-start | bytes 4260100
  7.2 299.7 %all-reduce.62.cloned.1.call-start = ((), (), s32[]{:S(2)}) async-start(), calls=%async_computation | async-start | bytes 352256 | tf_op jit(solution)/shard_map/psum | solution.py:12
  63.1 2.1 copy-start.5
  63.9 492.4 %all-reduce.64.cloned.1.call-start = ((), (), s32[]{:S(2)}) async-start(), calls=%async_computation.1 | async-start | bytes 352256 | tf_op jit(solution)/shard_map/psum | solution.py:12
  65.2 0.8 copy-start.46
  66.1 244.8 %copy-start.44 = (f32[2064]{0:T(1024)}, f32[2064]{0:T(1024)S(1)}, u32[]{:S(2)}) copy-start(f32[2064]{0:T(1024)S(1)} %fusion.173) | copy-start | bytes 24772
  66.5 241.4 %copy-start.4 = (f32[1,256,344]{1,2,0:T(8,128)}, f32[1,256,344]{1,2,0:T(8,128)S(1)}, u32[]{:S(2)}) copy-start(f32[1,256,344]{1,2,0:T(8,128)S(1)} %copy.33) | copy-start | bytes 1056772
  68.1 245.9 %copy-start.8 = (f32[2064]{0:T(1024)}, f32[2064]{0:T(1024)S(1)}, u32[]{:S(2)}) copy-start(f32[2064]{0:T(1024)S(1)} %get-tuple-element.147) | copy-start | bytes 24772
  68.1 245.9 %copy-start.10 = (f32[2064]{0:T(1024)}, f32[2064]{0:T(1024)S(1)}, u32[]{:S(2)}) copy-start(f32[2064]{0:T(1024)S(1)} %get-tuple-element.148) | copy-start | bytes 24772
  68.1 245.9 %copy-start.12 = (f32[2064]{0:T(1024)}, f32[2064]{0:T(1024)S(1)}, u32[]{:S(2)}) copy-start(f32[2064]{0:T(1024)S(1)} %get-tuple-element.149) | copy-start | bytes 24772
  68.1 245.9 %copy-start.14 = (f32[2064]{0:T(1024)}, f32[2064]{0:T(1024)S(1)}, u32[]{:S(2)}) copy-start(f32[2064]{0:T(1024)S(1)} %get-tuple-element.150) | copy-start | bytes 24772
  68.1 245.9 %copy-start.16 = (f32[2064]{0:T(1024)}, f32[2064]{0:T(1024)S(1)}, u32[]{:S(2)}) copy-start(f32[2064]{0:T(1024)S(1)} %get-tuple-element.143) | copy-start | bytes 24772
  68.1 245.9 %copy-start.18 = (f32[2064]{0:T(1024)}, f32[2064]{0:T(1024)S(1)}, u32[]{:S(2)}) copy-start(f32[2064]{0:T(1024)S(1)} %get-tuple-element.151) | copy-start | bytes 24772
  68.1 245.9 %copy-start.20 = (f32[2064]{0:T(1024)}, f32[2064]{0:T(1024)S(1)}, u32[]{:S(2)}) copy-start(f32[2064]{0:T(1024)S(1)} %get-tuple-element.152) | copy-start | bytes 24772
  68.1 245.9 %copy-start.22 = (f32[2064]{0:T(1024)}, f32[2064]{0:T(1024)S(1)}, u32[]{:S(2)}) copy-start(f32[2064]{0:T(1024)S(1)} %get-tuple-element.153) | copy-start | bytes 24772
  68.1 245.9 %copy-start.24 = (f32[2064]{0:T(1024)}, f32[2064]{0:T(1024)S(1)}, u32[]{:S(2)}) copy-start(f32[2064]{0:T(1024)S(1)} %get-tuple-element.154) | copy-start | bytes 24772
  68.1 245.9 %copy-start.26 = (f32[2064]{0:T(1024)}, f32[2064]{0:T(1024)S(1)}, u32[]{:S(2)}) copy-start(f32[2064]{0:T(1024)S(1)} %get-tuple-element.155) | copy-start | bytes 24772
  68.1 245.9 %copy-start.28 = (f32[2064]{0:T(1024)}, f32[2064]{0:T(1024)S(1)}, u32[]{:S(2)}) copy-start(f32[2064]{0:T(1024)S(1)} %get-tuple-element.156) | copy-start | bytes 24772
  68.2 245.9 %copy-start.30 = (f32[2064]{0:T(1024)}, f32[2064]{0:T(1024)S(1)}, u32[]{:S(2)}) copy-start(f32[2064]{0:T(1024)S(1)} %get-tuple-element.157) | copy-start | bytes 24772
  68.2 245.9 %copy-start.32 = (f32[2064]{0:T(1024)}, f32[2064]{0:T(1024)S(1)}, u32[]{:S(2)}) copy-start(f32[2064]{0:T(1024)S(1)} %get-tuple-element.158) | copy-start | bytes 24772
  68.2 245.9 %copy-start.34 = (f32[2064]{0:T(1024)}, f32[2064]{0:T(1024)S(1)}, u32[]{:S(2)}) copy-start(f32[2064]{0:T(1024)S(1)} %get-tuple-element.159) | copy-start | bytes 24772
  307.9 3.1 copy-start.6
  310.9 2.0 copy-start.2
  313.9 413.0 %all-reduce.66.cloned.1.call-start = ((), (), s32[]{:S(2)}) async-start(), calls=%async_computation.2 | async-start | bytes 6423552
  556.2 2.2 copy-start.3
  568.2 6.8 copy-start.17
  568.2 6.8 copy-start.19
  568.2 6.8 copy-start.21
  568.2 6.8 copy-start.23
  568.2 6.8 copy-start.25
  568.3 6.8 copy-start.27
  568.3 6.8 copy-start.29
  568.3 6.8 copy-start.31
  568.3 6.8 copy-start.33
  568.3 6.8 copy-start.35
  568.3 6.8 copy-start.36
  568.3 6.8 copy-start.37
  568.3 6.8 copy-start.38
  568.3 6.8 copy-start.39
  568.4 6.8 copy-start.40
  568.4 6.8 copy-start.41
  568.4 6.8 copy-start.42
  568.4 6.8 copy-start.43
  575.2 13.0 %copy-start.9 = (f32[2064]{0:T(1024)S(1)}, f32[2064]{0:T(1024)}, u32[]{:S(2)}) copy-start(f32[2064]{0:T(1024)} %copy-done.8) | copy-start | bytes 24772
  575.2 13.0 %copy-start.11 = (f32[2064]{0:T(1024)S(1)}, f32[2064]{0:T(1024)}, u32[]{:S(2)}) copy-start(f32[2064]{0:T(1024)} %copy-done.10) | copy-start | bytes 24772
  575.2 13.0 %copy-start.13 = (f32[2064]{0:T(1024)S(1)}, f32[2064]{0:T(1024)}, u32[]{:S(2)}) copy-start(f32[2064]{0:T(1024)} %copy-done.12) | copy-start | bytes 24772
  575.2 13.0 %copy-start.15 = (f32[2064]{0:T(1024)S(1)}, f32[2064]{0:T(1024)}, u32[]{:S(2)}) copy-start(f32[2064]{0:T(1024)} %copy-done.14) | copy-start | bytes 24772
  593.8 2.2 copy-start.47
  620.4 2.0 copy-start.7
  620.4 2.0 copy-start.45
  626.3 0.7 copy-start.50
  626.3 105.9 %copy-start.1 = (bf16[1,344,2064]{2,1,0:T(8,128)(2,1)S(1)}, bf16[1,344,2064]{2,1,0:T(8,128)(2,1)}, u32[]{:S(2)}) copy-start(bf16[1,344,2064]{2,1,0:T(8,128)(2,1)} %param.21) | copy-start | bytes 4260100
Sparse Core Ops, SparseCore 0:
  64.0 242.8 all-reduce.61
  314.0 242.1 all-reduce.63
  626.4 100.4 all-reduce.65
where the time goes:
time: 741 us; the launch traced here: 739 us
  waiting for transfers between devices  570 us (77%)
  other arithmetic  68.4 us (9%)
  blocking collectives  53.8 us (7%)
  between operations  18.6 us (3%)
  local copies, waits for them, and re-layouts  14.7 us (2%)
  matrix products  13.1 us (2%)
    psum x2, waiting for transfers between devices, spread(): return lax.psum(block, axis)  471 us
    unnamed x4, waiting for transfers between devices  98.8 us
    all_gather x1, blocking collectives, body(): maps_zero = lax.all_gather(first_maps, 'cand', axis=1, tiled=True)  35.9 us
    add_any x2, other arithmetic, apply_block(): padded[:, tap_row:tap_row + H, tap_col:tap_col + H, :]  23.3 us
    mul x2, other arithmetic, apply_block(): tap_weights[tap_row * 5 + tap_col]  18.5 us
    pmin x1, blocking collectives, body(): lax.pmin((jnp.where(layer_here == 0, cand_index, beyond), jnp.where(layer...  17.8 us
  transfers between devices with their start and end apart: 3, of which 3 were waited for; matrix products, arithmetic and copies ran while one was open for 2% of the time, Pallas kernels for 0%

commit v1 on v0

v1 whole, which is shorter than its diff:
```python
import functools

import jax
import jax.numpy as jnp
from jax import lax
from jax.experimental import pallas as pl
from jax.experimental.pallas import tpu as pltpu
from jax.sharding import PartitionSpec as P

C = 344
HID = 2064
H = 16
CELLS = 256
CHUNK = 256
FULL = HID // CHUNK
REST = HID - FULL * CHUNK
TILES = 2 * FULL + 1
INNER = (6, 7, 8, 11, 12, 13, 16, 17, 18)
F32 = jnp.float32
BF16 = jnp.bfloat16
MESH = pl.DeviceIdType.MESH


def sigmoid(v):
    return 0.5 * jnp.tanh(0.5 * v) + 0.5


def shift_columns(grid, b, col):
    if b == 0:
        return grid
    flat = pltpu.roll(grid.reshape(CELLS, 128), (-b) % CELLS, 0)
    moved = flat.reshape(H, H, 128)
    keep = col < H - b if b > 0 else col >= -b
    return jnp.where(keep, moved, 0.0)


def depthwise(e, tap):
    col = lax.broadcasted_iota(jnp.int32, (H, H, 128), 1)
    grid = e.reshape(H, H, 128)
    zero = jnp.zeros((2, H, 128), F32)
    total = None
    for b in range(-2, 3):
        moved = jnp.concatenate([zero, shift_columns(grid, b, col), zero], 0)
        for a in range(5):
            term = tap(5 * a + b + 2)[None, None, :] * moved[a : a + H]
            total = term if total is None else total + term
    return total.reshape(CELLS, 128)


def kernel(
    n_cand,
    n_img,
    x_ref,
    layer_ref,
    expand_ref,
    radius_ref,
    tu_hbm,
    tk_hbm,
    td_hbm,
    cu_hbm,
    ck_hbm,
    cd_hbm,
    gu_ref,
    gk_ref,
    gd_ref,
    tu,
    tk,
    td,
    cu,
    ck,
    cd,
    left_u,
    left_d,
    left_k,
    xg,
    x0,
    xb,
    xt,
    acc,
    acc2,
    eb,
    ebt,
    e_s,
    sp_s,
    sk_s,
    g_s,
    p_s,
    rows,
    kg,
    send_d,
    send_u,
    send_h,
    recv_d,
    recv_u,
    recv_h,
    w_sem,
    xs_sem,
    xr_sem,
    ss_sem,
    rs_sem,
):
    me_c = lax.axis_index("cand")
    me_i = lax.axis_index("img")

    copies = []
    for layer in range(2):
        for src, dst in ((tu_hbm, tu), (tk_hbm, tk), (td_hbm, td)):
            copies.append(pltpu.make_async_copy(src.at[layer], dst.at[layer], w_sem.at[len(copies)]))
    for src, dst in ((cu_hbm, cu), (ck_hbm, ck), (cd_hbm, cd)):
        copies.append(pltpu.make_async_copy(src.at[0], dst, w_sem.at[len(copies)]))
    for copy in copies:
        copy.start()

    barrier = pltpu.get_barrier_semaphore()

    def greet_cand(k, carry):
        peer = lax.rem(me_c + k, n_cand)
        pl.semaphore_signal(barrier, inc=1, device_id={"cand": peer}, device_id_type=MESH)
        return carry

    def greet_img(k, carry):
        peer = lax.rem(me_i + k, n_img)
        pl.semaphore_signal(barrier, inc=1, device_id={"img": peer}, device_id_type=MESH)
        return carry

    lax.fori_loop(1, n_cand, greet_cand, 0)
    lax.fori_loop(1, n_img, greet_img, 0)
    pl.semaphore_wait(barrier, n_cand + n_img - 2)

    def map_copy(k):
        peer = lax.rem(me_c + k, n_cand)
        return pltpu.make_async_remote_copy(
            src_ref=x_ref,
            dst_ref=xg.at[me_c],
            send_sem=xs_sem.at[k],
            recv_sem=xr_sem.at[me_c],
            device_id={"cand": peer},
            device_id_type=MESH,
        )

    def map_arrival(k):
        source = lax.rem(me_c + k, n_cand)
        return pltpu.make_async_remote_copy(
            src_ref=x_ref,
            dst_ref=xg.at[source],
            send_sem=xs_sem.at[k],
            recv_sem=xr_sem.at[source],
            device_id={"cand": source},
            device_id_type=MESH,
        )

    def start_map(k, carry):
        map_copy(k).start()
        return carry

    def wait_map(k, carry):
        map_arrival(k).wait_recv()
        return carry

    def wait_sent(k, carry):
        map_copy(k).wait_send()
        return carry

    lax.fori_loop(1, n_cand, start_map, 0)
    xg[me_c] = x_ref[...]

    rows[...] = jnp.zeros_like(rows)
    kg[...] = jnp.zeros_like(kg)
    left_u[...] = jnp.zeros_like(left_u)
    left_d[...] = jnp.zeros_like(left_d)
    left_k[...] = jnp.zeros_like(left_k)

    layer_here = layer_ref[0]
    units_used = expand_ref[0] * (HID // 2)
    outer = jnp.where(radius_ref[0] >= 2, 1.0, 0.0).astype(F32)

    def tap_mask(shape):
        row = lax.broadcasted_iota(jnp.int32, shape, 0)
        inner = row == INNER[0]
        for other in INNER[1:]:
            inner = inner | (row == other)
        return jnp.where(inner, 1.0, outer)

    def unit_mask(tile):
        lane = lax.broadcasted_iota(jnp.int32, (1, 128), 1) + tile * 128
        return jnp.where(lane < units_used, 1.0, 0.0)

    def lanes(j):
        return pl.ds(pl.multiple_of(j * CHUNK, CHUNK), CHUNK)

    def tile_lanes(tile):
        return pl.ds(pl.multiple_of(tile * 128, 128), 128)

    def teacher(layer, inputs, total):
        copies[3 * layer].wait()
        copies[3 * layer + 1].wait()
        copies[3 * layer + 2].wait()
        left_u[layer, :, :REST] = tu[layer, :, FULL * CHUNK :]
        left_d[layer, :, :REST] = td[layer, :, FULL * CHUNK :]
        left_k[layer, :25, :REST] = tk[layer, :, FULL * CHUNK :]

        def active(p, tap):
            k = depthwise(p * sigmoid(p), tap)
            return (k * sigmoid(k)).astype(BF16)

        p = jnp.dot(inputs[...], left_u[layer], preferred_element_type=F32)
        g = active(p, lambda i: left_k[layer, i, :])
        total[...] = lax.dot_general(
            g, left_d[layer], (((1,), (1,)), ((), ())), preferred_element_type=F32
        )

        def step(j, carry):
            p_s[...] = jnp.dot(inputs[...], tu[layer, :, lanes(j)], preferred_element_type=F32)
            for half in range(2):
                part = slice(128 * half, 128 * half + 128)
                tile = 2 * j + half
                g_s[FULL, :, part] = active(
                    p_s[:, part], lambda i: tk[layer, i, tile_lanes(tile)]
                )
            total[...] += lax.dot_general(
                g_s[FULL], td[layer, :, lanes(j)], (((1,), (1,)), ((), ())), preferred_element_type=F32
            )
            return carry

        lax.fori_loop(0, FULL, step, 0)

    lax.fori_loop(1, n_cand, wait_map, 0)
    x_wide = xg[...].astype(F32).reshape(CELLS, C)
    x0[...] = x_wide
    xb[...] = x_wide.astype(BF16)
    teacher(0, xb, acc)

    ones = x0[...] + acc[...]
    xb[...] = ones.astype(BF16)
    teacher(1, xb, acc2)
    first = layer_here == 0
    wide = jnp.where(first, x0[...], x0[...] + acc[...])
    xb[...] = wide.astype(BF16)
    acc[...] = jnp.where(first, acc[...], acc2[...])
    pad = jnp.zeros((CELLS, 384 - C), F32)
    xt[...] = jnp.transpose(jnp.concatenate([wide, pad], 1))[:C].astype(BF16)

    for copy in copies[6:]:
        copy.wait()
    ck[...] = ck[...] * tap_mask((25, HID))
    left_u[2, :, :REST] = cu[:, FULL * CHUNK :]
    left_d[2, :, :REST] = cd[:, FULL * CHUNK :]
    left_k[2, :25, :REST] = ck[:, FULL * CHUNK :]

    def forward_tile(p, tile, tap):
        mask = unit_mask(tile)
        s = sigmoid(p) * mask
        e = p * s
        e_s[tile] = e
        sp_s[tile] = s + e * (1.0 - s)
        k = depthwise(e, tap)
        s2 = sigmoid(k)
        g = k * s2
        sk_s[tile] = s2 + g * (1.0 - s2)
        return g.astype(BF16)

    p = jnp.dot(xb[...], left_u[2], preferred_element_type=F32)
    g = forward_tile(p, 2 * FULL, lambda i: left_k[2, i, :])
    g_s[FULL, :, :128] = g
    acc2[...] = lax.dot_general(g, left_d[2], (((1,), (1,)), ((), ())), preferred_element_type=F32)

    def forward(j, carry):
        p_s[...] = jnp.dot(xb[...], cu[:, lanes(j)], preferred_element_type=F32)
        for half in range(2):
            part = slice(128 * half, 128 * half + 128)
            tile = 2 * j + half
            g_s[j, :, part] = forward_tile(
                p_s[:, part], tile, lambda i: ck[i, tile_lanes(tile)]
            )
        acc2[...] += lax.dot_general(
            g_s[j], cd[:, lanes(j)], (((1,), (1,)), ((), ())), preferred_element_type=F32
        )
        return carry

    lax.fori_loop(0, FULL, forward, 0)

    error = (acc2[...] - acc[...]) * (1.0 / n_img)
    eb[...] = error.astype(BF16)
    ebt[...] = jnp.transpose(jnp.concatenate([error, pad], 1))[:C].astype(BF16)

    def grad_copy(kind, peer, slot, source):
        src, dst = ((send_d, recv_d), (send_u, recv_u), (send_h, recv_h))[kind]
        return pltpu.make_async_remote_copy(
            src_ref=src.at[slot],
            dst_ref=dst.at[source],
            send_sem=ss_sem.at[kind, slot],
            recv_sem=rs_sem.at[kind, source],
            device_id={"img": peer},
            device_id_type=MESH,
        )

    def head(block, other):
        turned = jnp.transpose(block)[:REST].astype(BF16)
        return jnp.dot(turned, other, preferred_element_type=F32).astype(BF16)

    def down_step(t, carry):
        j = lax.rem(me_i + n_img - t, n_img)
        send_d[j] = jnp.dot(ebt[...], g_s[j], preferred_element_type=F32).astype(BF16)
        before = lax.rem(j + n_img - 1, n_img)

        @pl.when(j > 0)
        def _():
            send_h[before, :REST, :C] = head(g_s[j, :, :128].astype(F32), eb[...])

        @pl.when(t > 0)
        def _():
            grad_copy(0, j, j, me_i).start()

        return carry

    send_h[n_img - 1, :REST, :C] = head(g_s[FULL, :, :128].astype(F32), eb[...])
    lax.fori_loop(0, n_img, down_step, 0)
    recv_d[me_i] = send_d[me_i]

    def backward_tile(dg, tile, tap):
        col = lax.broadcasted_iota(jnp.int32, (H, H, 128), 1)
        grid = (dg * sk_s[tile]).reshape(H, H, 128)
        for b in range(-2, 3):
            rows[b + 2, 2 : 2 + H] = shift_columns(grid, -b, col)
        total = [None] * H
        for b in range(-2, 3):
            sums = [None] * 5
            for r in range(H):
                e = e_s[tile, H * r : H * r + H, :]
                for a in range(-2, 3):
                    moved = rows[b + 2, 2 - a + r]
                    term = tap(5 * (a + 2) + b + 2)[None, :] * moved
                    total[r] = term if total[r] is None else total[r] + term
                    q = moved * e
                    q = q[:8] + q[8:]
                    sums[a + 2] = q if sums[a + 2] is None else sums[a + 2] + q
            for a in range(5):
                kg[5 * a + b + 2, :] = jnp.sum(sums[a], axis=0)
        de = jnp.concatenate(total, 0)
        return de * sp_s[tile]

    taps = tap_mask((32, 128))

    dg = jnp.dot(eb[...], left_d[2], preferred_element_type=F32)
    dp = backward_tile(dg, 2 * FULL, lambda i: left_k[2, i, :])
    send_h[n_img - 1, REST : 2 * REST, :C] = head(dp, xb[...])
    send_h[n_img - 1, 32:64, 256:384] = (kg[...] * taps).astype(BF16)

    def up_step(t, carry):
        j = lax.rem(me_i + n_img - t, n_img)
        before = lax.rem(j + n_img - 1, n_img)
        p_s[...] = jnp.dot(eb[...], cd[:, lanes(j)], preferred_element_type=F32)
        for half in range(2):
            part = slice(128 * half, 128 * half + 128)
            tile = 2 * j + half
            dp = backward_tile(p_s[:, part], tile, lambda i: ck[i, tile_lanes(tile)])
            dk = (kg[...] * taps).astype(BF16)
            send_h[j, 32:64, part] = dk
            p_s[:, part] = dp
            if half == 0:

                @pl.when(j > 0)
                def _():
                    send_h[before, REST : 2 * REST, :C] = head(p_s[:, :128], xb[...])
                    send_h[before, 32:64, 256:384] = dk

        send_u[j] = jnp.dot(xt[...], p_s[...].astype(BF16), preferred_element_type=F32).astype(BF16)

        @pl.when(t > 0)
        def _():
            grad_copy(1, j, j, me_i).start()
            grad_copy(2, j, j, me_i).start()

        return carry

    lax.fori_loop(0, n_img, up_step, 0)
    recv_u[me_i] = send_u[me_i]
    recv_h[me_i] = send_h[me_i]

    def arrivals(k, carry):
        source = lax.rem(me_i + k, n_img)
        for kind in range(3):
            grad_copy(kind, source, source, source).wait_recv()
        return carry

    lax.fori_loop(1, n_img, arrivals, 0)

    heads = recv_h[0].astype(F32)
    for source in range(1, n_img):
        heads = heads + recv_h[source].astype(F32)
    amount = lax.rem(384 - 2 * me_i, 384)
    wide_zero = jnp.zeros((128 - REST, 384), F32)

    def assemble(recv, head_rows, out):
        main = recv[0].astype(F32)
        for source in range(1, n_img):
            main = main + recv[source].astype(F32)
        tail = jnp.transpose(jnp.concatenate([head_rows, wide_zero], 0))[:C]
        whole = pltpu.roll(jnp.concatenate([main, tail], 1), amount, 1)
        out[...] = whole[:, : CHUNK + 2]

    assemble(recv_d, heads[:REST], gd_ref)
    assemble(recv_u, heads[REST : 2 * REST], gu_ref)
    gk_ref[...] = pltpu.roll(heads[32:64], amount, 1)[:25, : CHUNK + 2]

    lax.fori_loop(1, n_cand, wait_sent, 0)

    def sent(k, carry):
        peer = lax.rem(me_i + k, n_img)
        for kind in range(3):
            grad_copy(kind, peer, peer, me_i).wait_send()
        return carry

    lax.fori_loop(1, n_img, sent, 0)


def body(n_cand, n_img, first_maps, layer_of, expand_half, radius, *weights):
    teach_up, teach_dw, teach_down, cand_up, cand_dw, cand_down = weights
    vmem = pl.BlockSpec(memory_space=pltpu.VMEM)
    smem = pl.BlockSpec(memory_space=pltpu.SMEM)
    hbm = pl.BlockSpec(memory_space=pl.ANY)
    own = CHUNK + 2
    grads = pl.pallas_call(
        functools.partial(kernel, n_cand, n_img),
        out_shape=(
            jax.ShapeDtypeStruct((C, own), F32),
            jax.ShapeDtypeStruct((25, own), F32),
            jax.ShapeDtypeStruct((C, own), F32),
        ),
        in_specs=[vmem, smem, smem, smem] + [hbm] * 6,
        out_specs=(vmem, vmem, vmem),
        scratch_shapes=[
            pltpu.VMEM((2, C, HID), BF16),
            pltpu.VMEM((2, 25, HID), F32),
            pltpu.VMEM((2, C, HID), BF16),
            pltpu.VMEM((C, HID), BF16),
            pltpu.VMEM((25, HID), F32),
            pltpu.VMEM((C, HID), BF16),
            pltpu.VMEM((3, C, 128), BF16),
            pltpu.VMEM((3, C, 128), BF16),
            pltpu.VMEM((3, 32, 128), F32),
            pltpu.VMEM((n_cand, 8, C), BF16),
            pltpu.VMEM((CELLS, C), F32),
            pltpu.VMEM((CELLS, C), BF16),
            pltpu.VMEM((C, CELLS), BF16),
            pltpu.VMEM((CELLS, C), F32),
            pltpu.VMEM((CELLS, C), F32),
            pltpu.VMEM((CELLS, C), BF16),
            pltpu.VMEM((C, CELLS), BF16),
            pltpu.VMEM((TILES, CELLS, 128), F32),
            pltpu.VMEM((TILES, CELLS, 128), F32),
            pltpu.VMEM((TILES, CELLS, 128), F32),
            pltpu.VMEM((FULL + 1, CELLS, CHUNK), BF16),
            pltpu.VMEM((CELLS, CHUNK), F32),
            pltpu.VMEM((5, H + 4, H, 128), F32),
            pltpu.VMEM((32, 128), F32),
            pltpu.VMEM((n_img, C, CHUNK), BF16),
            pltpu.VMEM((n_img, C, CHUNK), BF16),
            pltpu.VMEM((n_img, 64, 384), BF16),
            pltpu.VMEM((n_img, C, CHUNK), BF16),
            pltpu.VMEM((n_img, C, CHUNK), BF16),
            pltpu.VMEM((n_img, 64, 384), BF16),
            pltpu.SemaphoreType.DMA((9,)),
            pltpu.SemaphoreType.DMA((n_cand,)),
            pltpu.SemaphoreType.DMA((n_cand,)),
            pltpu.SemaphoreType.DMA((3, n_img)),
            pltpu.SemaphoreType.DMA((3, n_img)),
        ],
        compiler_params=pltpu.CompilerParams(
            collective_id=0, has_side_effects=True, vmem_limit_bytes=56 * 1024 * 1024
        ),
        name="step",
    )(
        first_maps[0].astype(BF16),
        layer_of,
        expand_half,
        radius,
        teach_up,
        teach_dw,
        teach_down,
        cand_up,
        cand_dw,
        cand_down,
    )
    return tuple(grad[None] for grad in grads)


def solution(mesh):
    placed = (
        P("img", "cand", None),
        P("cand"),
        P("cand"),
        P("cand"),
        P(),
        P(),
        P(),
        P("cand", None, None),
        P("cand", None, None),
        P("cand", None, None),
    )
    return jax.shard_map(
        functools.partial(body, mesh.shape["cand"], mesh.shape["img"]),
        mesh=mesh,
        in_specs=placed,
        out_specs=(P("cand", None, "img"), P("cand", None, "img"), P("cand", None, "img")),
        check_vma=False,
    )
```

time: 741 us -> 110 us (0.15)
  the two profiles are of different devices: /device:TPU:1 before, /device:TPU:6 now
where the time goes in v1:
time: 110 us
  Pallas kernels  97 us (88%)
  local copies, waits for them, and re-layouts  8.99 us (8%)
  between operations  2.58 us (2%)
  other arithmetic  1.3 us (1%)
    pallas_call x1, Pallas kernels, body(): pl.pallas_call(functools.partial(kernel, n_cand, n_img), out_shape=(jax.S...  97 us
    unnamed x5, local copies, waits for them, and re-layouts  8.99 us

profile of v1, /device:TPU:6, one launch (start us, length us, event | category | flops | bytes accessed | tf_op | source)
XLA Modules:
  0.0 109.8 jit_solution(2527616160412873832)
XLA Ops:
  2.6 1.3 %convert_bitcast_fusion.x_ref = bf16[8,344]{1,0:T(8,128)(2,1)} fusion(f32[1,8,344]{2,1,0:T(8,128)} %param.10), kind=kLoop, calls=%fused_computation | loop fusion | flops 2752 | bytes 16512 | tf_op jit(solution)/shard_map/convert_element_type | solution.py:474
  3.9 1.7 %copy.14.ck_hbm = f32[1,25,2064]{2,1,0:T(8,128)} copy(f32[1,25,2064]{2,0,1:T(1,128)} %param.18) | data formatting | bytes 412800 | tf_op args[8]
  5.5 1.9 %copy.13.tk_hbm = f32[2,25,2064]{2,1,0:T(8,128)} copy(f32[2,25,2064]{2,0,1:T(2,128)} %param.15) | data formatting | bytes 825600 | tf_op args[5]
  7.4 97.0 %step.1 = (f32[344,258]{1,0:T(8,128)}, f32[25,258]{1,0:T(8,128)}, f32[344,258]{1,0:T(8,128)}) custom-call(bf16[8,344]{1,0:T(8,128)(2,1)} %convert_bitcast_fusion.x_ref, s32[1]{0:T(128)S(6)} %copy.18.layer_ref, s32[1]{0:T(128)S(6)} %copy.19.expand_ref, s32[1]{0:T(128)S(6)} %copy.20.radius_ref, bf16[2,344,2064]{2,1,0:T(8,128)(2,1)} %tu_hbm.1, ...), custom_call_target="tpu_custom_call" | custom-call | tf_op jit(solution)/shard_map/step/pallas_call | solution.py:423
  104.4 2.0 %copy.15 = f32[1,344,258]{1,0,2:T(1,128)} copy(f32[1,344,258]{2,1,0:T(8,128)} %bitcast.6) | data formatting | bytes 710016
  106.4 1.5 %copy.16 = f32[1,25,258]{2,0,1:T(1,128)} copy(f32[1,25,258]{2,1,0:T(8,128)} %bitcast.7) | data formatting | bytes 51600
  107.8 2.0 %copy.17 = f32[1,344,258]{1,0,2:T(1,128)} copy(f32[1,344,258]{2,1,0:T(8,128)} %bitcast.5) | data formatting | bytes 710016

commit v2 on v1

--- a/solution.py
+++ b/solution.py
@@ -45,6 +45,28 @@
             term = tap(5 * a + b + 2)[None, None, :] * moved[a : a + H]
             total = term if total is None else total + term
     return total.reshape(CELLS, 128)
+
+
+def depthwise_row(e, tap):
+    col = lax.broadcasted_iota(jnp.int32, (5, H, 128), 1)
+    total = None
+    for b in range(-2, 3):
+        if b == 0:
+            moved = e.reshape(5, H, 128)
+        else:
+            moved = pltpu.roll(e, (-b) % (5 * H), 0).reshape(5, H, 128)
+            moved = jnp.where(col < H - b if b > 0 else col >= -b, moved, 0.0)
+        for a in range(5):
+            term = tap(5 * a + b + 2)[None, :] * moved[a]
+            total = term if total is None else total + term
+    return total
+
+
+def finish(gu_ref, gk_ref, gd_ref, up_ref, dw_ref, down_ref):
+    own = CHUNK + 2
+    for src, dst in ((gu_ref, up_ref), (gd_ref, down_ref)):
+        dst[:, 0, :] = jnp.transpose(src[...])[:own, :C]
+    dw_ref[:, 0, :] = gk_ref[:25, :own]
 
 
 def kernel(
@@ -98,19 +120,29 @@
     xr_sem,
     ss_sem,
     rs_sem,
+    base,
+    xpad,
+    xh,
+    row_out,
+    row_in,
+    pair_sem,
+    ts_sem,
+    tr_sem,
 ):
     me_c = lax.axis_index("cand")
     me_i = lax.axis_index("img")
 
     copies = []
     for layer in range(2):
-        for src, dst in ((tu_hbm, tu), (tk_hbm, tk), (td_hbm, td)):
+        for src, dst in ((tu_hbm, tu), (td_hbm, td)):
             copies.append(pltpu.make_async_copy(src.at[layer], dst.at[layer], w_sem.at[len(copies)]))
-    for src, dst in ((cu_hbm, cu), (ck_hbm, ck), (cd_hbm, cd)):
-        copies.append(pltpu.make_async_copy(src.at[0], dst, w_sem.at[len(copies)]))
+    copies.insert(0, pltpu.make_async_copy(tk_hbm, tk, w_sem.at[len(copies)]))
+    for src, dst in ((cu_hbm.at[0], cu), (ck_hbm, ck), (cd_hbm.at[0], cd)):
+        copies.append(pltpu.make_async_copy(src, dst, w_sem.at[len(copies)]))
     for copy in copies:
         copy.start()
 
+    xh[...] = x_ref[0].astype(BF16)
     barrier = pltpu.get_barrier_semaphore()
 
     def greet_cand(k, carry):
@@ -130,7 +162,7 @@
     def map_copy(k):
         peer = lax.rem(me_c + k, n_cand)
         return pltpu.make_async_remote_copy(
-            src_ref=x_ref,
+            src_ref=xh,
             dst_ref=xg.at[me_c],
             send_sem=xs_sem.at[k],
             recv_sem=xr_sem.at[me_c],
@@ -141,7 +173,7 @@
     def map_arrival(k):
         source = lax.rem(me_c + k, n_cand)
         return pltpu.make_async_remote_copy(
-            src_ref=x_ref,
+            src_ref=xh,
             dst_ref=xg.at[source],
             send_sem=xs_sem.at[k],
             recv_sem=xr_sem.at[source],
@@ -162,9 +194,10 @@
         return carry
 
     lax.fori_loop(1, n_cand, start_map, 0)
-    xg[me_c] = x_ref[...]
+    xg[me_c] = xh[...]
 
     rows[...] = jnp.zeros_like(rows)
+    xpad[...] = jnp.zeros_like(xpad)
     kg[...] = jnp.zeros_like(kg)
     left_u[...] = jnp.zeros_like(left_u)
     left_d[...] = jnp.zeros_like(left_d)
@@ -191,61 +224,150 @@
     def tile_lanes(tile):
         return pl.ds(pl.multiple_of(tile * 128, 128), 128)
 
-    def teacher(layer, inputs, total):
-        copies[3 * layer].wait()
-        copies[3 * layer + 1].wait()
-        copies[3 * layer + 2].wait()
+    def active(p, conv):
+        k = conv(p * sigmoid(p))
+        return (k * sigmoid(k)).astype(BF16)
+
+    def whole_map(tap):
+        return lambda e: depthwise(e, tap)
+
+    def one_row(tap):
+        return lambda e: depthwise_row(e, tap)
+
+    def load_left(layer):
         left_u[layer, :, :REST] = tu[layer, :, FULL * CHUNK :]
         left_d[layer, :, :REST] = td[layer, :, FULL * CHUNK :]
-        left_k[layer, :25, :REST] = tk[layer, :, FULL * CHUNK :]
-
-        def active(p, tap):
-            k = depthwise(p * sigmoid(p), tap)
-            return (k * sigmoid(k)).astype(BF16)
-
-        p = jnp.dot(inputs[...], left_u[layer], preferred_element_type=F32)
-        g = active(p, lambda i: left_k[layer, i, :])
-        total[...] = lax.dot_general(
-            g, left_d[layer], (((1,), (1,)), ((), ())), preferred_element_type=F32
-        )
-
-        def step(j, carry):
-            p_s[...] = jnp.dot(inputs[...], tu[layer, :, lanes(j)], preferred_element_type=F32)
+        left_k[layer, :25, :REST] = tk[:, layer, FULL * CHUNK :]
+
+    core = lax.rem(me_c, 2)
+    map_row = me_c // 2
+
+    def teacher_first():
+        for copy in copies[:3]:
+            copy.wait()
+        load_left(0)
+        p = jnp.dot(xb[...], left_u[0], preferred_element_type=F32)
+        g = active(p, whole_map(lambda i: left_k[0, i, :]))
+        rest = lax.dot_general(g, left_d[0], (((1,), (1,)), ((), ())), preferred_element_type=F32)
+        acc[...] = jnp.where(core == 0, rest, 0.0)
+
+        def step(t, carry):
+            j = core * (FULL // 2) + t
+            p_s[...] = jnp.dot(xb[...], tu[0, :, lanes(j)], preferred_element_type=F32)
             for half in range(2):
                 part = slice(128 * half, 128 * half + 128)
                 tile = 2 * j + half
                 g_s[FULL, :, part] = active(
-                    p_s[:, part], lambda i: tk[layer, i, tile_lanes(tile)]
+                    p_s[:, part], whole_map(lambda i: tk[i, 0, tile_lanes(tile)])
                 )
-            total[...] += lax.dot_general(
-                g_s[FULL], td[layer, :, lanes(j)], (((1,), (1,)), ((), ())), preferred_element_type=F32
+            acc[...] += lax.dot_general(
+                g_s[FULL], td[0, :, lanes(j)], (((1,), (1,)), ((), ())), preferred_element_type=F32
             )
             return carry
 
-        lax.fori_loop(0, FULL, step, 0)
+        lax.fori_loop(0, FULL // 2, step, 0)
+
+    def pair_copy():
+        return pltpu.make_async_remote_copy(
+            src_ref=acc,
+            dst_ref=acc2,
+            send_sem=pair_sem.at[0],
+            recv_sem=pair_sem.at[1],
+            device_id={"cand": me_c + 1 - 2 * core},
+            device_id_type=MESH,
+        )
+
+    def teacher_row():
+        for copy in copies[3:5]:
+            copy.wait()
+        load_left(1)
+        near = xpad[pl.ds(pl.multiple_of(map_row * H, H), 5 * H), :]
+        p = jnp.dot(near, left_u[1], preferred_element_type=F32)
+        g = active(p, one_row(lambda i: left_k[1, i, :]))
+        rest = lax.dot_general(g, left_d[1], (((1,), (1,)), ((), ())), preferred_element_type=F32)
+
+        def step(j, total):
+            p = jnp.dot(
+                xpad[pl.ds(pl.multiple_of(map_row * H, H), 5 * H), :],
+                tu[1, :, lanes(j)],
+                preferred_element_type=F32,
+            )
+            parts = []
+            for half in range(2):
+                tile = 2 * j + half
+                parts.append(
+                    active(
+                        p[:, 128 * half : 128 * half + 128],
+                        one_row(lambda i: tk[i, 1, tile_lanes(tile)]),
+                    )
+                )
+            return total + lax.dot_general(
+                jnp.concatenate(parts, 1),
+                td[1, :, lanes(j)],
+                (((1,), (1,)), ((), ())),
+                preferred_element_type=F32,
+            )
+
+        row_out[...] = lax.fori_loop(0, FULL, step, rest).astype(BF16)
+
+    def row_copy(k):
+        peer = lax.rem(me_c + 2 * k, n_cand)
+        return pltpu.make_async_remote_copy(
+            src_ref=row_out,
+            dst_ref=row_in.at[map_row],
+            send_sem=ts_sem.at[k],
+            recv_sem=tr_sem.at[map_row],
+            device_id={"cand": peer},
+            device_id_type=MESH,
+        )
+
+    def row_arrival(k):
+        source = lax.rem(map_row + k, H)
+        return pltpu.make_async_remote_copy(
+            src_ref=row_out,
+            dst_ref=row_in.at[source],
+            send_sem=ts_sem.at[k],
+            recv_sem=tr_sem.at[source],
+            device_id={"cand": lax.rem(me_c + 2 * k, n_cand)},
+            device_id_type=MESH,
+        )
+
+    def start_row(k, carry):
+        row_copy(k).start()
+        return carry
+
+    def wait_row(k, carry):
+        row_arrival(k).wait_recv()
+        return carry
+
+    def sent_row(k, carry):
+        row_copy(k).wait_send()
+        return carry
 
     lax.fori_loop(1, n_cand, wait_map, 0)
     x_wide = xg[...].astype(F32).reshape(CELLS, C)
     x0[...] = x_wide
     xb[...] = x_wide.astype(BF16)
-    teacher(0, xb, acc)
-
-    ones = x0[...] + acc[...]
-    xb[...] = ones.astype(BF16)
-    teacher(1, xb, acc2)
+    teacher_first()
+    pair = pair_copy()
+    pair.start()
+    pair.wait()
+    ones = x0[...] + (acc[...] + acc2[...])
+    base[...] = acc[...] + acc2[...]
+    xpad[2 * H : 2 * H + CELLS] = ones.astype(BF16)
+    teacher_row()
     first = layer_here == 0
-    wide = jnp.where(first, x0[...], x0[...] + acc[...])
+    wide = jnp.where(first, x0[...], ones)
     xb[...] = wide.astype(BF16)
-    acc[...] = jnp.where(first, acc[...], acc2[...])
     pad = jnp.zeros((CELLS, 384 - C), F32)
     xt[...] = jnp.transpose(jnp.concatenate([wide, pad], 1))[:C].astype(BF16)
 
-    for copy in copies[6:]:
+    for copy in copies[5:]:
         copy.wait()
-    ck[...] = ck[...] * tap_mask((25, HID))
+    ck[...] = ck[...] * tap_mask((25, 1, HID))
     left_u[2, :, :REST] = cu[:, FULL * CHUNK :]
     left_d[2, :, :REST] = cd[:, FULL * CHUNK :]
-    left_k[2, :25, :REST] = ck[:, FULL * CHUNK :]
+    left_k[2, :25, :REST] = ck[:, 0, FULL * CHUNK :]
 
     def forward_tile(p, tile, tap):
         mask = unit_mask(tile)
@@ -264,13 +386,16 @@
     g_s[FULL, :, :128] = g
     acc2[...] = lax.dot_general(g, left_d[2], (((1,), (1,)), ((), ())), preferred_element_type=F32)
 
+    lax.fori_loop(1, H, start_row, 0)
+    row_in[map_row] = row_out[...]
+
     def forward(j, carry):
         p_s[...] = jnp.dot(xb[...], cu[:, lanes(j)], preferred_element_type=F32)
         for half in range(2):
             part = slice(128 * half, 128 * half + 128)
             tile = 2 * j + half
             g_s[j, :, part] = forward_tile(
-                p_s[:, part], tile, lambda i: ck[i, tile_lanes(tile)]
+                p_s[:, part], tile, lambda i: ck[i, 0, tile_lanes(tile)]
             )
         acc2[...] += lax.dot_general(
             g_s[j], cd[:, lanes(j)], (((1,), (1,)), ((), ())), preferred_element_type=F32
@@ -279,7 +404,9 @@
 
     lax.fori_loop(0, FULL, forward, 0)
 
-    error = (acc2[...] - acc[...]) * (1.0 / n_img)
+    lax.fori_loop(1, H, wait_row, 0)
+    second = row_in[...].astype(F32).reshape(CELLS, C)
+    error = (acc2[...] - jnp.where(first, base[...], second)) * (1.0 / n_img)
     eb[...] = error.astype(BF16)
     ebt[...] = jnp.transpose(jnp.concatenate([error, pad], 1))[:C].astype(BF16)
 
@@ -353,7 +480,7 @@
         for half in range(2):
             part = slice(128 * half, 128 * half + 128)
             tile = 2 * j + half
-            dp = backward_tile(p_s[:, part], tile, lambda i: ck[i, tile_lanes(tile)])
+            dp = backward_tile(p_s[:, part], tile, lambda i: ck[i, 0, tile_lanes(tile)])
             dk = (kg[...] * taps).astype(BF16)
             send_h[j, 32:64, part] = dk
             p_s[:, part] = dp
@@ -397,13 +524,15 @@
             main = main + recv[source].astype(F32)
         tail = jnp.transpose(jnp.concatenate([head_rows, wide_zero], 0))[:C]
         whole = pltpu.roll(jnp.concatenate([main, tail], 1), amount, 1)
-        out[...] = whole[:, : CHUNK + 2]
+        out[:C, :] = whole
+        out[C:, :] = jnp.zeros((384 - C, 384), F32)
 
     assemble(recv_d, heads[:REST], gd_ref)
     assemble(recv_u, heads[REST : 2 * REST], gu_ref)
-    gk_ref[...] = pltpu.roll(heads[32:64], amount, 1)[:25, : CHUNK + 2]
+    gk_ref[...] = pltpu.roll(heads[32:64], amount, 1)
 
     lax.fori_loop(1, n_cand, wait_sent, 0)
+    lax.fori_loop(1, H, sent_row, 0)
 
     def sent(k, carry):
         peer = lax.rem(me_i + k, n_img)
@@ -423,18 +552,18 @@
     grads = pl.pallas_call(
         functools.partial(kernel, n_cand, n_img),
         out_shape=(
-            jax.ShapeDtypeStruct((C, own), F32),
-            jax.ShapeDtypeStruct((25, own), F32),
-            jax.ShapeDtypeStruct((C, own), F32),
+            jax.ShapeDtypeStruct((384, 384), F32),
+            jax.ShapeDtypeStruct((32, 384), F32),
+            jax.ShapeDtypeStruct((384, 384), F32),
         ),
         in_specs=[vmem, smem, smem, smem] + [hbm] * 6,
         out_specs=(vmem, vmem, vmem),
         scratch_shapes=[
             pltpu.VMEM((2, C, HID), BF16),
-            pltpu.VMEM((2, 25, HID), F32),
+            pltpu.VMEM((25, 2, HID), F32),
             pltpu.VMEM((2, C, HID), BF16),
             pltpu.VMEM((C, HID), BF16),
-            pltpu.VMEM((25, HID), F32),
+            pltpu.VMEM((25, 1, HID), F32),
             pltpu.VMEM((C, HID), BF16),
             pltpu.VMEM((3, C, 128), BF16),
             pltpu.VMEM((3, C, 128), BF16),
@@ -465,24 +594,48 @@
             pltpu.SemaphoreType.DMA((n_cand,)),
             pltpu.SemaphoreType.DMA((3, n_img)),
             pltpu.SemaphoreType.DMA((3, n_img)),
+            pltpu.VMEM((CELLS, C), F32),
+            pltpu.VMEM((CELLS + 4 * H, C), BF16),
+            pltpu.VMEM((8, C), BF16),
+            pltpu.VMEM((H, C), BF16),
+            pltpu.VMEM((H, H, C), BF16),
+            pltpu.SemaphoreType.DMA((2,)),
+            pltpu.SemaphoreType.DMA((H,)),
+            pltpu.SemaphoreType.DMA((H,)),
         ],
         compiler_params=pltpu.CompilerParams(
             collective_id=0, has_side_effects=True, vmem_limit_bytes=56 * 1024 * 1024
         ),
         name="step",
     )(
-        first_maps[0].astype(BF16),
+        first_maps,
         layer_of,
         expand_half,
         radius,
         teach_up,
-        teach_dw,
+        jnp.transpose(teach_dw, (1, 0, 2)),
         teach_down,
         cand_up,
-        cand_dw,
+        jnp.transpose(cand_dw, (1, 0, 2)),
         cand_down,
     )
-    return tuple(grad[None] for grad in grads)
+    up, dw, down = pl.pallas_call(
+        finish,
+        out_shape=(
+            jax.ShapeDtypeStruct((own, 1, C), F32),
+            jax.ShapeDtypeStruct((25, 1, own), F32),
+            jax.ShapeDtypeStruct((own, 1, C), F32),
+        ),
+        in_specs=[vmem] * 3,
+        out_specs=(vmem, vmem, vmem),
+        compiler_params=pltpu.CompilerParams(vmem_limit_bytes=8 * 1024 * 1024),
+        name="finish",
+    )(*grads)
+    return (
+        jnp.transpose(up, (1, 2, 0)),
+        jnp.transpose(dw, (1, 0, 2)),
+        jnp.transpose(down, (1, 2, 0)),
+    )
 
 
 def solution(mesh):

time: 110 us -> 97.5 us (0.89)
  local copies, waits for them, and re-layouts: 8.99 us -> 2.92 us
  Pallas kernels: 97 us -> 91.7 us
  other arithmetic: 1.3 us -> 0 us
    pallas_call x1, Pallas kernels: 97 us -> 90.5 us  [body(): pl.pallas_call(functools.partial(kernel, n_cand, n_img), out_shape=(jax.S...]
    unnamed x5 -> x6, local copies, waits for them, and re-layouts: 8.99 us -> 2.92 us
    convert_element_type x1 -> x0, other arithmetic: 1.3 us -> none  [body(): first_maps[0].astype(BF16)]
    pallas_call x0 -> x1, Pallas kernels: none -> 1.17 us  [body(): pl.pallas_call(finish, out_shape=(jax.ShapeDtypeStruct((own, 1, C), F32),...]
where the time goes in v2:
time: 97.5 us; the launch traced here: 97.2 us
  Pallas kernels  91.7 us (94%)
  local copies, waits for them, and re-layouts  2.92 us (3%)
  between operations  2.59 us (3%)
    pallas_call x1, Pallas kernels, body(): pl.pallas_call(functools.partial(kernel, n_cand, n_img), out_shape=(jax.S...  90.5 us
    unnamed x6, local copies, waits for them, and re-layouts  2.92 us

profile of v2, /device:TPU:6, one launch (start us, length us, event | category | flops | bytes accessed | tf_op | source)
XLA Modules:
  0.0 97.2 jit_solution(765005164779072963)
XLA Ops:
  2.6 90.5 %step.1 = (f32[384,384]{1,0:T(8,128)}, f32[32,384]{1,0:T(8,128)}, f32[384,384]{1,0:T(8,128)}) custom-call(f32[1,8,344]{2,1,0:T(8,128)} %x_ref.1, s32[1]{0:T(128)S(6)} %copy.13.layer_ref, s32[1]{0:T(128)S(6)} %copy.14.expand_ref, s32[1]{0:T(128)S(6)} %copy.15.radius_ref, bf16[2,344,2064]{2,1,0:T(8,128)(2,1)} %tu_hbm.1, f32[25,2,2064]{2,1,0:T(2,128)} %bitcast.5, ...), custom_call_target="tpu_custom_call" | custom-call | tf_op jit(solution)/shard_map/step/pallas_call | solution.py:552
  93.1 0.0 copy-start
  93.1 1.1 %copy-done = f32[384,384]{1,0:T(8,128)S(1)} copy-done((f32[384,384]{1,0:T(8,128)S(1)}, f32[384,384]{1,0:T(8,128)}, u32[]{:S(2)}) %copy-start) | copy-done | bytes 589848
  94.2 0.0 copy-start.1
  94.2 1.1 %copy-done.1 = f32[384,384]{1,0:T(8,128)S(1)} copy-done((f32[384,384]{1,0:T(8,128)S(1)}, f32[384,384]{1,0:T(8,128)}, u32[]{:S(2)}) %copy-start.1) | copy-done | bytes 589848
  95.2 0.0 copy-start.2
  95.2 0.8 copy-done.2
  96.0 1.2 %finish.1 = (f32[258,1,344]{2,1,0:T(1,128)}, f32[25,1,258]{2,1,0:T(1,128)}, f32[258,1,344]{2,1,0:T(1,128)}) custom-call(f32[384,384]{1,0:T(8,128)S(1)} %copy-done, f32[32,384]{1,0:T(8,128)S(1)} %copy-done.2, f32[384,384]{1,0:T(8,128)S(1)} %copy-done.1), custom_call_target="tpu_custom_call" | custom-call | tf_op jit(solution)/shard_map/finish/pallas_call | solution.py:622
Async XLA Ops:
  93.1 1.1 %copy-start = (f32[384,384]{1,0:T(8,128)S(1)}, f32[384,384]{1,0:T(8,128)}, u32[]{:S(2)}) copy-start(f32[384,384]{1,0:T(8,128)} %get-tuple-element.9.gu_ref) | copy-start | bytes 1769476
  94.2 1.1 %copy-start.1 = (f32[384,384]{1,0:T(8,128)S(1)}, f32[384,384]{1,0:T(8,128)}, u32[]{:S(2)}) copy-start(f32[384,384]{1,0:T(8,128)} %get-tuple-element.11.gd_ref) | copy-start | bytes 1769476
  95.2 0.8 copy-start.2

commit v3 on v2

--- a/solution.py
+++ b/solution.py
@@ -15,6 +15,9 @@
 FULL = HID // CHUNK
 REST = HID - FULL * CHUNK
 TILES = 2 * FULL + 1
+X = 4
+DOWN_ROWS = 384
+UP_ROWS = 448
 INNER = (6, 7, 8, 11, 12, 13, 16, 17, 18)
 F32 = jnp.float32
 BF16 = jnp.bfloat16
@@ -62,11 +65,20 @@
     return total
 
 
-def finish(gu_ref, gk_ref, gd_ref, up_ref, dw_ref, down_ref):
+def finish(gu_hbm, gk_hbm, gd_hbm, up_ref, dw_ref, down_ref, gu, gk, gd, sem):
     own = CHUNK + 2
-    for src, dst in ((gu_ref, up_ref), (gd_ref, down_ref)):
-        dst[:, 0, :] = jnp.transpose(src[...])[:own, :C]
-    dw_ref[:, 0, :] = gk_ref[:25, :own]
+    copies = [
+        pltpu.make_async_copy(src, dst, sem.at[k])
+        for k, (src, dst) in enumerate(((gu_hbm, gu), (gk_hbm, gk), (gd_hbm, gd)))
+    ]
+    for copy in copies:
+        copy.start()
+    copies[0].wait()
+    up_ref[:, 0, :] = jnp.transpose(gu[...])[:own, :C]
+    copies[1].wait()
+    dw_ref[:, 0, :] = gk[:25, :own]
+    copies[2].wait()
+    down_ref[:, 0, :] = jnp.transpose(gd[...])[:own, :C]
 
 
 def kernel(
@@ -109,17 +121,19 @@
     p_s,
     rows,
     kg,
-    send_d,
-    send_u,
-    send_h,
-    recv_d,
-    recv_u,
-    recv_h,
+    down_own,
+    down_y,
+    down_sum,
+    down_x,
+    up_own,
+    up_x,
+    up_sum,
+    up_y,
     w_sem,
     xs_sem,
     xr_sem,
-    ss_sem,
-    rs_sem,
+    down_sem,
+    up_sem,
     base,
     xpad,
     xh,
@@ -215,8 +229,13 @@
         return jnp.where(inner, 1.0, outer)
 
     def unit_mask(tile):
-        lane = lax.broadcasted_iota(jnp.int32, (1, 128), 1) + tile * 128
-        return jnp.where(lane < units_used, 1.0, 0.0)
+        unit = lax.broadcasted_iota(jnp.int32, (1, 128), 1) + tile * 128
+        return jnp.where(unit < units_used, 1.0, 0.0)
+
+    def border_mask():
+        place = lax.broadcasted_iota(jnp.int32, (1, 128), 1)
+        unit = ((place >> 4) + 1) * CHUNK + (place & 15)
+        return jnp.where(unit < units_used, 1.0, 0.0)
 
     def lanes(j):
         return pl.ds(pl.multiple_of(j * CHUNK, CHUNK), CHUNK)
@@ -243,9 +262,6 @@
     map_row = me_c // 2
 
     def teacher_first():
-        for copy in copies[:3]:
-            copy.wait()
-        load_left(0)
         p = jnp.dot(xb[...], left_u[0], preferred_element_type=F32)
         g = active(p, whole_map(lambda i: left_k[0, i, :]))
         rest = lax.dot_general(g, left_d[0], (((1,), (1,)), ((), ())), preferred_element_type=F32)
@@ -278,9 +294,6 @@
         )
 
     def teacher_row():
-        for copy in copies[3:5]:
-            copy.wait()
-        load_left(1)
         near = xpad[pl.ds(pl.multiple_of(map_row * H, H), 5 * H), :]
         p = jnp.dot(near, left_u[1], preferred_element_type=F32)
         g = active(p, one_row(lambda i: left_k[1, i, :]))
@@ -344,6 +357,39 @@
         row_copy(k).wait_send()
         return carry
 
+    for copy in copies:
+        copy.wait()
+    load_left(0)
+    load_left(1)
+    ck[...] = ck[...] * tap_mask((25, 1, HID))
+    lane = lax.broadcasted_iota(jnp.int32, (1, 128), 1)
+
+    def borders(block, rows_of):
+        whole = jnp.zeros((rows_of, 128), F32)
+        for k in range(n_img):
+            part = block(k + 1).astype(F32)
+            part = part if k == 0 else pltpu.roll(part, REST * k, 1)
+            whole = jnp.where((lane >> 4) == k, part, whole)
+        return whole
+
+    def wide_tile(ref, k):
+        if k == FULL:
+            return jnp.concatenate([ref[:, FULL * CHUNK :], jnp.zeros((C, 128 - REST), BF16)], 1)
+        return ref[:, k * CHUNK : k * CHUNK + 128]
+
+    def tap_tile(k):
+        if k == FULL:
+            return jnp.concatenate(
+                [ck[:, 0, FULL * CHUNK :], jnp.zeros((25, 128 - REST), F32)], 1
+            )
+        return ck[:, 0, k * CHUNK : k * CHUNK + 128]
+
+    left_u[2] = borders(lambda k: wide_tile(cu, k), C).astype(BF16)
+    edge_down = borders(lambda k: wide_tile(cd, k), C)
+    left_d[2] = edge_down.astype(BF16)
+    left_d[3] = jnp.where(lane >= 128 - REST, edge_down, 0.0).astype(BF16)
+    left_k[2, :25] = borders(tap_tile, 25)
+
     lax.fori_loop(1, n_cand, wait_map, 0)
     x_wide = xg[...].astype(F32).reshape(CELLS, C)
     x0[...] = x_wide
@@ -362,15 +408,7 @@
     pad = jnp.zeros((CELLS, 384 - C), F32)
     xt[...] = jnp.transpose(jnp.concatenate([wide, pad], 1))[:C].astype(BF16)
 
-    for copy in copies[5:]:
-        copy.wait()
-    ck[...] = ck[...] * tap_mask((25, 1, HID))
-    left_u[2, :, :REST] = cu[:, FULL * CHUNK :]
-    left_d[2, :, :REST] = cd[:, FULL * CHUNK :]
-    left_k[2, :25, :REST] = ck[:, 0, FULL * CHUNK :]
-
-    def forward_tile(p, tile, tap):
-        mask = unit_mask(tile)
+    def forward_tile(p, tile, tap, mask):
         s = sigmoid(p) * mask
         e = p * s
         e_s[tile] = e
@@ -382,9 +420,9 @@
         return g.astype(BF16)
 
     p = jnp.dot(xb[...], left_u[2], preferred_element_type=F32)
-    g = forward_tile(p, 2 * FULL, lambda i: left_k[2, i, :])
+    g = forward_tile(p, 2 * FULL, lambda i: left_k[2, i, :], border_mask())
     g_s[FULL, :, :128] = g
-    acc2[...] = lax.dot_general(g, left_d[2], (((1,), (1,)), ((), ())), preferred_element_type=F32)
+    acc2[...] = lax.dot_general(g, left_d[3], (((1,), (1,)), ((), ())), preferred_element_type=F32)
 
     lax.fori_loop(1, H, start_row, 0)
     row_in[map_row] = row_out[...]
@@ -395,7 +433,7 @@
             part = slice(128 * half, 128 * half + 128)
             tile = 2 * j + half
             g_s[j, :, part] = forward_tile(
-                p_s[:, part], tile, lambda i: ck[i, 0, tile_lanes(tile)]
+                p_s[:, part], tile, lambda i: ck[i, 0, tile_lanes(tile)], unit_mask(tile)
             )
         acc2[...] += lax.dot_general(
             g_s[j], cd[:, lanes(j)], (((1,), (1,)), ((), ())), preferred_element_type=F32
@@ -410,39 +448,89 @@
     eb[...] = error.astype(BF16)
     ebt[...] = jnp.transpose(jnp.concatenate([error, pad], 1))[:C].astype(BF16)
 
-    def grad_copy(kind, peer, slot, source):
-        src, dst = ((send_d, recv_d), (send_u, recv_u), (send_h, recv_h))[kind]
+    my_x = lax.rem(me_i, X)
+    my_y = me_i // X
+
+    def send(src, dst, sems, peer):
         return pltpu.make_async_remote_copy(
-            src_ref=src.at[slot],
-            dst_ref=dst.at[source],
-            send_sem=ss_sem.at[kind, slot],
-            recv_sem=rs_sem.at[kind, source],
+            src_ref=src,
+            dst_ref=dst,
+            send_sem=sems[0],
+            recv_sem=sems[1],
             device_id={"img": peer},
             device_id_type=MESH,
         )
 
-    def head(block, other):
-        turned = jnp.transpose(block)[:REST].astype(BF16)
-        return jnp.dot(turned, other, preferred_element_type=F32).astype(BF16)
-
-    def down_step(t, carry):
-        j = lax.rem(me_i + n_img - t, n_img)
-        send_d[j] = jnp.dot(ebt[...], g_s[j], preferred_element_type=F32).astype(BF16)
-        before = lax.rem(j + n_img - 1, n_img)
-
-        @pl.when(j > 0)
-        def _():
-            send_h[before, :REST, :C] = head(g_s[j, :, :128].astype(F32), eb[...])
-
-        @pl.when(t > 0)
-        def _():
-            grad_copy(0, j, j, me_i).start()
-
-        return carry
-
-    send_h[n_img - 1, :REST, :C] = head(g_s[FULL, :, :128].astype(F32), eb[...])
-    lax.fori_loop(0, n_img, down_step, 0)
-    recv_d[me_i] = send_d[me_i]
+    def down_over_y(x):
+        slab = X * (1 - my_y) + x
+        return send(
+            down_own.at[slab],
+            down_y.at[x],
+            (down_sem.at[0, 0, x], down_sem.at[0, 1, x]),
+            X * (1 - my_y) + my_x,
+        )
+
+    def down_over_x(x, source):
+        return send(
+            down_sum.at[x],
+            down_x.at[source],
+            (down_sem.at[1, 0, x], down_sem.at[1, 1, source]),
+            X * my_y + x,
+        )
+
+    def up_over_x(y, x, source):
+        return send(
+            up_own.at[X * y + x],
+            up_x.at[y, source],
+            (up_sem.at[0, y, x], up_sem.at[1, y, source]),
+            X * my_y + x,
+        )
+
+    def up_over_y():
+        return send(
+            up_sum, up_y, (up_sem.at[0, 2, 0], up_sem.at[1, 2, 0]), X * (1 - my_y) + my_x
+        )
+
+    def turn(block, other):
+        return jnp.dot(
+            jnp.transpose(block).astype(BF16), other, preferred_element_type=F32
+        ).astype(BF16)
+
+    def place_heads(ref, heads):
+        for k in range(n_img):
+            part = slice(REST * k, REST * k + REST)
+            ref[k, 352:368, :] = heads[part, :CHUNK]
+            ref[k, 368:384, : C - CHUNK] = heads[part, CHUNK:]
+
+    place_heads(down_own, turn(g_s[FULL, :, :128].astype(F32), eb[...]))
+
+    def down_slab(y, x):
+        j = X * y + x
+        down_own[j, :C] = jnp.dot(ebt[...], g_s[j], preferred_element_type=F32).astype(BF16)
+
+    order = (2, 1, 3, 0)
+
+    for k in order:
+        x = lax.rem(my_x + k, X)
+        down_slab(1 - my_y, x)
+        down_over_y(x).start()
+
+    def own_down(x, carry):
+        down_slab(my_y, x)
+        return carry
+
+    lax.fori_loop(0, X, own_down, 0)
+
+    def relay_down(x):
+        down_over_y(x).wait_recv()
+        down_sum[x] = (
+            down_own[X * my_y + x].astype(F32) + down_y[x].astype(F32)
+        ).astype(BF16)
+
+    def relay_and_send(k):
+        x = lax.rem(my_x + k, X)
+        relay_down(x)
+        down_over_x(x, my_x).start()
 
     def backward_tile(dg, tile, tap):
         col = lax.broadcasted_iota(jnp.int32, (H, H, 128), 1)
@@ -470,77 +558,98 @@
 
     dg = jnp.dot(eb[...], left_d[2], preferred_element_type=F32)
     dp = backward_tile(dg, 2 * FULL, lambda i: left_k[2, i, :])
-    send_h[n_img - 1, REST : 2 * REST, :C] = head(dp, xb[...])
-    send_h[n_img - 1, 32:64, 256:384] = (kg[...] * taps).astype(BF16)
+    place_heads(up_own, turn(dp, xb[...]))
+    edge = kg[...] * taps
+    for k in range(n_img):
+        moved = edge if k == 0 else pltpu.roll(edge, 128 - REST * k, 1)
+        up_own[k, 416:448, :128] = moved.astype(BF16)
 
     def up_step(t, carry):
-        j = lax.rem(me_i + n_img - t, n_img)
-        before = lax.rem(j + n_img - 1, n_img)
+        k = X - 1 - (t >> 1)
+        x = lax.rem(my_x + k, X)
+        y = lax.rem(my_y + 1 + t, 2)
+        j = X * y + x
         p_s[...] = jnp.dot(eb[...], cd[:, lanes(j)], preferred_element_type=F32)
         for half in range(2):
             part = slice(128 * half, 128 * half + 128)
             tile = 2 * j + half
-            dp = backward_tile(p_s[:, part], tile, lambda i: ck[i, 0, tile_lanes(tile)])
-            dk = (kg[...] * taps).astype(BF16)
-            send_h[j, 32:64, part] = dk
-            p_s[:, part] = dp
-            if half == 0:
-
-                @pl.when(j > 0)
-                def _():
-                    send_h[before, REST : 2 * REST, :C] = head(p_s[:, :128], xb[...])
-                    send_h[before, 32:64, 256:384] = dk
-
-        send_u[j] = jnp.dot(xt[...], p_s[...].astype(BF16), preferred_element_type=F32).astype(BF16)
-
-        @pl.when(t > 0)
+            p_s[:, part] = backward_tile(
+                p_s[:, part], tile, lambda i: ck[i, 0, tile_lanes(tile)]
+            )
+            up_own[j, 384:416, part] = (kg[...] * taps).astype(BF16)
+        up_own[j, :C] = jnp.dot(
+            xt[...], p_s[...].astype(BF16), preferred_element_type=F32
+        ).astype(BF16)
+
+        @pl.when(k > 0)
         def _():
-            grad_copy(1, j, j, me_i).start()
-            grad_copy(2, j, j, me_i).start()
+            up_over_x(y, x, my_x).start()
+
+        for when, which in ((3, 2), (5, 1), (7, 3)):
+
+            @pl.when(t == when)
+            def _():
+                relay_and_send(which)
 
         return carry
 
     lax.fori_loop(0, n_img, up_step, 0)
-    recv_u[me_i] = send_u[me_i]
-    recv_h[me_i] = send_h[me_i]
-
-    def arrivals(k, carry):
-        source = lax.rem(me_i + k, n_img)
-        for kind in range(3):
-            grad_copy(kind, source, source, source).wait_recv()
-        return carry
-
-    lax.fori_loop(1, n_img, arrivals, 0)
-
-    heads = recv_h[0].astype(F32)
-    for source in range(1, n_img):
-        heads = heads + recv_h[source].astype(F32)
+
+    def sum_x(y):
+        total = up_own[X * y + my_x].astype(F32)
+        for k in range(1, X):
+            source = lax.rem(my_x + k, X)
+            up_over_x(y, source, source).wait_recv()
+            total = total + up_x[y, source].astype(F32)
+        return total
+
+    up_sum[...] = sum_x(1 - my_y).astype(BF16)
+    up_over_y().start()
+    relay_down(my_x)
+
     amount = lax.rem(384 - 2 * me_i, 384)
     wide_zero = jnp.zeros((128 - REST, 384), F32)
-
-    def assemble(recv, head_rows, out):
-        main = recv[0].astype(F32)
-        for source in range(1, n_img):
-            main = main + recv[source].astype(F32)
-        tail = jnp.transpose(jnp.concatenate([head_rows, wide_zero], 0))[:C]
-        whole = pltpu.roll(jnp.concatenate([main, tail], 1), amount, 1)
-        out[:C, :] = whole
+    lane_zero = jnp.zeros((REST, 384 - C), F32)
+
+    def assemble(total, out):
+        heads = jnp.concatenate([total[352:368], total[368:384, : C - CHUNK], lane_zero], 1)
+        tail = jnp.transpose(jnp.concatenate([heads, wide_zero], 0))[:C]
+        out[:C, :] = pltpu.roll(jnp.concatenate([total[:C], tail], 1), amount, 1)
         out[C:, :] = jnp.zeros((384 - C, 384), F32)
 
-    assemble(recv_d, heads[:REST], gd_ref)
-    assemble(recv_u, heads[REST : 2 * REST], gu_ref)
-    gk_ref[...] = pltpu.roll(heads[32:64], amount, 1)
+    total = down_sum[my_x].astype(F32)
+    for k in range(1, X):
+        source = lax.rem(my_x + k, X)
+        down_over_x(source, source).wait_recv()
+        total = total + down_x[source].astype(F32)
+    assemble(total, gd_ref)
+
+    total = sum_x(my_y)
+    up_over_y().wait_recv()
+    total = total + up_y[...].astype(F32)
+    assemble(total, gu_ref)
+    gk_ref[...] = pltpu.roll(
+        jnp.concatenate([total[384:416], total[416:448, :128]], 1), amount, 1
+    )
 
     lax.fori_loop(1, n_cand, wait_sent, 0)
     lax.fori_loop(1, H, sent_row, 0)
 
-    def sent(k, carry):
-        peer = lax.rem(me_i + k, n_img)
-        for kind in range(3):
-            grad_copy(kind, peer, peer, me_i).wait_send()
-        return carry
-
-    lax.fori_loop(1, n_img, sent, 0)
+    def sent_y(x, carry):
+        down_over_y(x).wait_send()
+        return carry
+
+    lax.fori_loop(0, X, sent_y, 0)
+
+    def sent_x(k, carry):
+        x = lax.rem(my_x + k, X)
+        down_over_x(x, my_x).wait_send()
+        up_over_x(0, x, my_x).wait_send()
+        up_over_x(1, x, my_x).wait_send()
+        return carry
+
+    lax.fori_loop(1, X, sent_x, 0)
+    up_over_y().wait_send()
 
 
 def body(n_cand, n_img, first_maps, layer_of, expand_half, radius, *weights):
@@ -566,7 +675,7 @@
             pltpu.VMEM((25, 1, HID), F32),
             pltpu.VMEM((C, HID), BF16),
             pltpu.VMEM((3, C, 128), BF16),
-            pltpu.VMEM((3, C, 128), BF16),
+            pltpu.VMEM((4, C, 128), BF16),
             pltpu.VMEM((3, 32, 128), F32),
             pltpu.VMEM((n_cand, 8, C), BF16),
             pltpu.VMEM((CELLS, C), F32),
@@ -583,17 +692,19 @@
             pltpu.VMEM((CELLS, CHUNK), F32),
             pltpu.VMEM((5, H + 4, H, 128), F32),
             pltpu.VMEM((32, 128), F32),
-            pltpu.VMEM((n_img, C, CHUNK), BF16),
-            pltpu.VMEM((n_img, C, CHUNK), BF16),
-            pltpu.VMEM((n_img, 64, 384), BF16),
-            pltpu.VMEM((n_img, C, CHUNK), BF16),
-            pltpu.VMEM((n_img, C, CHUNK), BF16),
-            pltpu.VMEM((n_img, 64, 384), BF16),
+            pltpu.VMEM((n_img, DOWN_ROWS, CHUNK), BF16),
+            pltpu.VMEM((X, DOWN_ROWS, CHUNK), BF16),
+            pltpu.VMEM((X, DOWN_ROWS, CHUNK), BF16),
+            pltpu.VMEM((X, DOWN_ROWS, CHUNK), BF16),
+            pltpu.VMEM((n_img, UP_ROWS, CHUNK), BF16),
+            pltpu.VMEM((2, X, UP_ROWS, CHUNK), BF16),
+            pltpu.VMEM((UP_ROWS, CHUNK), BF16),
+            pltpu.VMEM((UP_ROWS, CHUNK), BF16),
             pltpu.SemaphoreType.DMA((9,)),
             pltpu.SemaphoreType.DMA((n_cand,)),
             pltpu.SemaphoreType.DMA((n_cand,)),
-            pltpu.SemaphoreType.DMA((3, n_img)),
-            pltpu.SemaphoreType.DMA((3, n_img)),
+            pltpu.SemaphoreType.DMA((2, 2, X)),
+            pltpu.SemaphoreType.DMA((2, 3, X)),
             pltpu.VMEM((CELLS, C), F32),
             pltpu.VMEM((CELLS + 4 * H, C), BF16),
             pltpu.VMEM((8, C), BF16),
@@ -626,8 +737,14 @@
             jax.ShapeDtypeStruct((25, 1, own), F32),
             jax.ShapeDtypeStruct((own, 1, C), F32),
         ),
-        in_specs=[vmem] * 3,
+        in_specs=[hbm] * 3,
         out_specs=(vmem, vmem, vmem),
+        scratch_shapes=[
+            pltpu.VMEM((384, 384), F32),
+            pltpu.VMEM((32, 384), F32),
+            pltpu.VMEM((384, 384), F32),
+            pltpu.SemaphoreType.DMA((3,)),
+        ],
         compiler_params=pltpu.CompilerParams(vmem_limit_bytes=8 * 1024 * 1024),
         name="finish",
     )(*grads)

time: 97.5 us -> 87.8 us (0.901)
  the two profiles are of different devices: /device:TPU:6 before, /device:TPU:1 now
where the time goes in v3:
time: 87.8 us; the launch traced here: 87.5 us
  Pallas kernels  82 us (93%)
  local copies, waits for them, and re-layouts  2.92 us (3%)
  between operations  2.59 us (3%)
    pallas_call x1, Pallas kernels, body(): pl.pallas_call(functools.partial(kernel, n_cand, n_img), out_shape=(jax.S...  80.4 us
    unnamed x6, local copies, waits for them, and re-layouts  2.92 us

profile of v3, /device:TPU:1, one launch (start us, length us, event | category | flops | bytes accessed | tf_op | source)
XLA Modules:
  0.0 87.5 jit_solution(14313998210705063455)
XLA Ops:
  2.6 80.4 %step.1 = (f32[384,384]{1,0:T(8,128)}, f32[32,384]{1,0:T(8,128)}, f32[384,384]{1,0:T(8,128)}) custom-call(f32[1,8,344]{2,1,0:T(8,128)} %x_ref.1, s32[1]{0:T(128)S(6)} %copy.13.layer_ref, s32[1]{0:T(128)S(6)} %copy.14.expand_ref, s32[1]{0:T(128)S(6)} %copy.15.radius_ref, bf16[2,344,2064]{2,1,0:T(8,128)(2,1)} %tu_hbm.1, f32[25,2,2064]{2,1,0:T(2,128)} %bitcast.5, ...), custom_call_target="tpu_custom_call" | custom-call | tf_op jit(solution)/shard_map/step/pallas_call | solution.py:661
  83.0 0.0 copy-start
  83.0 1.1 %copy-done = f32[384,384]{1,0:T(8,128)S(1)} copy-done((f32[384,384]{1,0:T(8,128)S(1)}, f32[384,384]{1,0:T(8,128)}, u32[]{:S(2)}) %copy-start) | copy-done | bytes 589848
  84.1 0.0 copy-start.1
  84.1 1.1 %copy-done.1 = f32[384,384]{1,0:T(8,128)S(1)} copy-done((f32[384,384]{1,0:T(8,128)S(1)}, f32[384,384]{1,0:T(8,128)}, u32[]{:S(2)}) %copy-start.1) | copy-done | bytes 589848
  85.1 0.0 copy-start.2
  85.1 0.8 copy-done.2
  85.9 1.6 %finish.1 = (f32[258,1,344]{2,1,0:T(1,128)}, f32[25,1,258]{2,1,0:T(1,128)}, f32[258,1,344]{2,1,0:T(1,128)}) custom-call(f32[384,384]{1,0:T(8,128)S(1)} %copy-done, f32[32,384]{1,0:T(8,128)S(1)} %copy-done.2, f32[384,384]{1,0:T(8,128)S(1)} %copy-done.1), custom_call_target="tpu_custom_call" | custom-call | tf_op jit(solution)/shard_map/finish/pallas_call | solution.py:733
Async XLA Ops:
  83.0 1.1 %copy-start = (f32[384,384]{1,0:T(8,128)S(1)}, f32[384,384]{1,0:T(8,128)}, u32[]{:S(2)}) copy-start(f32[384,384]{1,0:T(8,128)} %get-tuple-element.9.gu_hbm) | copy-start | bytes 1769476
  84.1 1.1 %copy-start.1 = (f32[384,384]{1,0:T(8,128)S(1)}, f32[384,384]{1,0:T(8,128)}, u32[]{:S(2)}) copy-start(f32[384,384]{1,0:T(8,128)} %get-tuple-element.11.gd_hbm) | copy-start | bytes 1769476
  85.1 0.8 copy-start.2

commit v4 on v3

--- a/solution.py
+++ b/solution.py
@@ -17,7 +17,10 @@
 TILES = 2 * FULL + 1
 X = 4
 DOWN_ROWS = 384
-UP_ROWS = 448
+UP_ROWS = 416
+PLACES = 1914
+SIDES = 166
+HALF = DOWN_ROWS // 2
 INNER = (6, 7, 8, 11, 12, 13, 16, 17, 18)
 F32 = jnp.float32
 BF16 = jnp.bfloat16
@@ -129,6 +132,8 @@
     up_x,
     up_sum,
     up_y,
+    down_relay,
+    up_relay,
     w_sem,
     xs_sem,
     xr_sem,
@@ -486,6 +491,25 @@
             X * my_y + x,
         )
 
+    def opposite(h):
+        return lax.rem(my_x + 3 - 2 * h, X)
+
+    def down_half(h):
+        return send(
+            down_sum.at[lax.rem(my_x + 2, X), pl.ds(HALF * h, HALF)],
+            down_relay.at[h],
+            (down_sem.at[2, 0, h], down_sem.at[2, 1, h]),
+            X * my_y + opposite(h),
+        )
+
+    def up_half(h):
+        return send(
+            up_own.at[X * h + lax.rem(my_x + 2, X)],
+            up_relay.at[h],
+            (up_sem.at[0, 2, 1 + h], up_sem.at[1, 2, 1 + h]),
+            X * my_y + opposite(h),
+        )
+
     def up_over_y():
         return send(
             up_sum, up_y, (up_sem.at[0, 2, 0], up_sem.at[1, 2, 0]), X * (1 - my_y) + my_x
@@ -508,7 +532,7 @@
         j = X * y + x
         down_own[j, :C] = jnp.dot(ebt[...], g_s[j], preferred_element_type=F32).astype(BF16)
 
-    order = (2, 1, 3, 0)
+    order = (2, 3, 1, 0)
 
     for k in order:
         x = lax.rem(my_x + k, X)
@@ -527,9 +551,19 @@
             down_own[X * my_y + x].astype(F32) + down_y[x].astype(F32)
         ).astype(BF16)
 
-    def relay_and_send(k):
-        x = lax.rem(my_x + k, X)
+    def split_down():
+        relay_down(lax.rem(my_x + 2, X))
+        for h in range(2):
+            down_half(h).start()
+
+    def join_down(h):
+        x = opposite(h)
         relay_down(x)
+        down_half(h).wait_recv()
+        part = slice(HALF * h, HALF * h + HALF)
+        down_sum[x, part] = (
+            down_sum[x, part].astype(F32) + down_relay[h].astype(F32)
+        ).astype(BF16)
         down_over_x(x, my_x).start()
 
     def backward_tile(dg, tile, tap):
@@ -562,12 +596,13 @@
     edge = kg[...] * taps
     for k in range(n_img):
         moved = edge if k == 0 else pltpu.roll(edge, 128 - REST * k, 1)
-        up_own[k, 416:448, :128] = moved.astype(BF16)
+        low = jnp.where(lane < REST, moved[:REST], pltpu.roll(moved[REST:], REST, 1))
+        up_own[k, 368:384, 128:] = low.astype(BF16)
 
     def up_step(t, carry):
-        k = X - 1 - (t >> 1)
+        k = (jnp.int32(PLACES) >> (2 * t)) & 3
         x = lax.rem(my_x + k, X)
-        y = lax.rem(my_y + 1 + t, 2)
+        y = (jnp.int32(SIDES) >> t) & 1
         j = X * y + x
         p_s[...] = jnp.dot(eb[...], cd[:, lanes(j)], preferred_element_type=F32)
         for half in range(2):
@@ -581,23 +616,36 @@
             xt[...], p_s[...].astype(BF16), preferred_element_type=F32
         ).astype(BF16)
 
-        @pl.when(k > 0)
+        @pl.when(t < 2)
+        def _():
+            up_half(t).start()
+
+        @pl.when((t == 4) | (t == 5))
+        def _():
+            h = t - 4
+            up_half(h).wait_recv()
+            up_own[j] = (up_own[j].astype(F32) + up_relay[h].astype(F32)).astype(BF16)
+
+        @pl.when((t >= 2) & (t < 6))
         def _():
             up_over_x(y, x, my_x).start()
 
-        for when, which in ((3, 2), (5, 1), (7, 3)):
-
-            @pl.when(t == when)
-            def _():
-                relay_and_send(which)
+        @pl.when(t == 3)
+        def _():
+            split_down()
+
+        @pl.when(t == 7)
+        def _():
+            join_down(0)
 
         return carry
 
     lax.fori_loop(0, n_img, up_step, 0)
+    join_down(1)
 
     def sum_x(y):
         total = up_own[X * y + my_x].astype(F32)
-        for k in range(1, X):
+        for k in (1, 3):
             source = lax.rem(my_x + k, X)
             up_over_x(y, source, source).wait_recv()
             total = total + up_x[y, source].astype(F32)
@@ -618,7 +666,7 @@
         out[C:, :] = jnp.zeros((384 - C, 384), F32)
 
     total = down_sum[my_x].astype(F32)
-    for k in range(1, X):
+    for k in (1, 3):
         source = lax.rem(my_x + k, X)
         down_over_x(source, source).wait_recv()
         total = total + down_x[source].astype(F32)
@@ -628,8 +676,10 @@
     up_over_y().wait_recv()
     total = total + up_y[...].astype(F32)
     assemble(total, gu_ref)
+    low = total[368:384, 128:]
+    edge = jnp.concatenate([low, pltpu.roll(low, 128 - REST, 1)], 0)
     gk_ref[...] = pltpu.roll(
-        jnp.concatenate([total[384:416], total[416:448, :128]], 1), amount, 1
+        jnp.concatenate([total[384:416], edge], 1), amount, 1
     )
 
     lax.fori_loop(1, n_cand, wait_sent, 0)
@@ -641,14 +691,14 @@
 
     lax.fori_loop(0, X, sent_y, 0)
 
-    def sent_x(k, carry):
+    for k in (1, 3):
         x = lax.rem(my_x + k, X)
         down_over_x(x, my_x).wait_send()
         up_over_x(0, x, my_x).wait_send()
         up_over_x(1, x, my_x).wait_send()
-        return carry
-
-    lax.fori_loop(1, X, sent_x, 0)
+    for h in range(2):
+        down_half(h).wait_send()
+        up_half(h).wait_send()
     up_over_y().wait_send()
 
 
@@ -700,10 +750,12 @@
             pltpu.VMEM((2, X, UP_ROWS, CHUNK), BF16),
             pltpu.VMEM((UP_ROWS, CHUNK), BF16),
             pltpu.VMEM((UP_ROWS, CHUNK), BF16),
+            pltpu.VMEM((2, HALF, CHUNK), BF16),
+            pltpu.VMEM((2, UP_ROWS, CHUNK), BF16),
             pltpu.SemaphoreType.DMA((9,)),
             pltpu.SemaphoreType.DMA((n_cand,)),
             pltpu.SemaphoreType.DMA((n_cand,)),
-            pltpu.SemaphoreType.DMA((2, 2, X)),
+            pltpu.SemaphoreType.DMA((3, 2, X)),
             pltpu.SemaphoreType.DMA((2, 3, X)),
             pltpu.VMEM((CELLS, C), F32),
             pltpu.VMEM((CELLS + 4 * H, C), BF16),
@@ -745,7 +797,7 @@
             pltpu.VMEM((384, 384), F32),
             pltpu.SemaphoreType.DMA((3,)),
         ],
-        compiler_params=pltpu.CompilerParams(vmem_limit_bytes=8 * 1024 * 1024),
+        compiler_params=pltpu.CompilerParams(vmem_limit_bytes=60 * 1024 * 1024),
         name="finish",
     )(*grads)
     return (

time: 87.8 us -> 75.7 us (0.86)
  Pallas kernels: 82 us -> 72.8 us
  local copies, waits for them, and re-layouts: 2.92 us -> 0 us
    pallas_call x1, Pallas kernels: 80.4 us -> 70.5 us  [body(): pl.pallas_call(functools.partial(kernel, n_cand, n_img), out_shape=(jax.S...]
    unnamed x6 -> x0, local copies, waits for them, and re-layouts: 2.92 us -> none
where the time goes in v4:
time: 75.7 us; the launch traced here: 75.4 us
  Pallas kernels  72.8 us (96%)
  between operations  2.58 us (3%)
    pallas_call x1, Pallas kernels, body(): pl.pallas_call(functools.partial(kernel, n_cand, n_img), out_shape=(jax.S...  70.5 us
    pallas_call x1, Pallas kernels, body(): pl.pallas_call(finish, out_shape=(jax.ShapeDtypeStruct((own, 1, C), F32),...  2.36 us

profile of v4, /device:TPU:1, one launch (start us, length us, event | category | flops | bytes accessed | tf_op | source)
XLA Modules:
  0.0 75.4 jit_solution(16774579472516635915)
XLA Ops:
  2.6 70.5 %step.1 = (f32[384,384]{1,0:T(8,128)}, f32[32,384]{1,0:T(8,128)}, f32[384,384]{1,0:T(8,128)}) custom-call(f32[1,8,344]{2,1,0:T(8,128)} %x_ref.1, s32[1]{0:T(128)S(6)} %copy.13.layer_ref, s32[1]{0:T(128)S(6)} %copy.14.expand_ref, s32[1]{0:T(128)S(6)} %copy.15.radius_ref, bf16[2,344,2064]{2,1,0:T(8,128)(2,1)} %tu_hbm.1, f32[25,2,2064]{2,1,0:T(2,128)} %bitcast.5, ...), custom_call_target="tpu_custom_call" | custom-call | tf_op jit(solution)/shard_map/step/pallas_call | solution.py:711
  73.0 2.4 %finish.1 = (f32[258,1,344]{2,1,0:T(1,128)}, f32[25,1,258]{2,1,0:T(1,128)}, f32[258,1,344]{2,1,0:T(1,128)}) custom-call(f32[384,384]{1,0:T(8,128)} %get-tuple-element.9.gu_hbm, f32[32,384]{1,0:T(8,128)} %get-tuple-element.10.gk_hbm, f32[384,384]{1,0:T(8,128)} %get-tuple-element.11.gd_hbm), custom_call_target="tpu_custom_call" | custom-call | tf_op jit(solution)/shard_map/finish/pallas_call | solution.py:785

commit v5 on v4

--- a/solution.py
+++ b/solution.py
@@ -19,6 +19,7 @@
 DOWN_ROWS = 384
 UP_ROWS = 416
 PLACES = 1914
+ROW_STEP = 4
 SIDES = 166
 HALF = DOWN_ROWS // 2
 INNER = (6, 7, 8, 11, 12, 13, 16, 17, 18)
@@ -134,6 +135,7 @@
     up_y,
     down_relay,
     up_relay,
+    g_t,
     w_sem,
     xs_sem,
     xr_sem,
@@ -274,12 +276,12 @@
 
         def step(t, carry):
             j = core * (FULL // 2) + t
-            p_s[...] = jnp.dot(xb[...], tu[0, :, lanes(j)], preferred_element_type=F32)
+            p_s[0] = jnp.dot(xb[...], tu[0, :, lanes(j)], preferred_element_type=F32)
             for half in range(2):
                 part = slice(128 * half, 128 * half + 128)
                 tile = 2 * j + half
                 g_s[FULL, :, part] = active(
-                    p_s[:, part], whole_map(lambda i: tk[i, 0, tile_lanes(tile)])
+                    p_s[0, :, part], whole_map(lambda i: tk[i, 0, tile_lanes(tile)])
                 )
             acc[...] += lax.dot_general(
                 g_s[FULL], td[0, :, lanes(j)], (((1,), (1,)), ((), ())), preferred_element_type=F32
@@ -304,29 +306,28 @@
         g = active(p, one_row(lambda i: left_k[1, i, :]))
         rest = lax.dot_general(g, left_d[1], (((1,), (1,)), ((), ())), preferred_element_type=F32)
 
-        def step(j, total):
-            p = jnp.dot(
-                xpad[pl.ds(pl.multiple_of(map_row * H, H), 5 * H), :],
-                tu[1, :, lanes(j)],
-                preferred_element_type=F32,
-            )
-            parts = []
-            for half in range(2):
-                tile = 2 * j + half
-                parts.append(
-                    active(
-                        p[:, 128 * half : 128 * half + 128],
-                        one_row(lambda i: tk[i, 1, tile_lanes(tile)]),
+        def step(m, total):
+            for k in range(ROW_STEP):
+                j = ROW_STEP * m + k
+                p = jnp.dot(near, tu[1, :, lanes(j)], preferred_element_type=F32)
+                parts = []
+                for half in range(2):
+                    tile = 2 * j + half
+                    parts.append(
+                        active(
+                            p[:, 128 * half : 128 * half + 128],
+                            one_row(lambda i, tile=tile: tk[i, 1, tile_lanes(tile)]),
+                        )
                     )
+                total = total + lax.dot_general(
+                    jnp.concatenate(parts, 1),
+                    td[1, :, lanes(j)],
+                    (((1,), (1,)), ((), ())),
+                    preferred_element_type=F32,
                 )
-            return total + lax.dot_general(
-                jnp.concatenate(parts, 1),
-                td[1, :, lanes(j)],
-                (((1,), (1,)), ((), ())),
-                preferred_element_type=F32,
-            )
-
-        row_out[...] = lax.fori_loop(0, FULL, step, rest).astype(BF16)
+            return total
+
+        row_out[...] = lax.fori_loop(0, FULL // ROW_STEP, step, rest).astype(BF16)
 
     def row_copy(k):
         peer = lax.rem(me_c + 2 * k, n_cand)
@@ -407,6 +408,8 @@
     base[...] = acc[...] + acc2[...]
     xpad[2 * H : 2 * H + CELLS] = ones.astype(BF16)
     teacher_row()
+    lax.fori_loop(1, H, start_row, 0)
+    row_in[map_row] = row_out[...]
     first = layer_here == 0
     wide = jnp.where(first, x0[...], ones)
     xb[...] = wide.astype(BF16)
@@ -429,23 +432,31 @@
     g_s[FULL, :, :128] = g
     acc2[...] = lax.dot_general(g, left_d[3], (((1,), (1,)), ((), ())), preferred_element_type=F32)
 
-    lax.fori_loop(1, H, start_row, 0)
-    row_in[map_row] = row_out[...]
-
-    def forward(j, carry):
-        p_s[...] = jnp.dot(xb[...], cu[:, lanes(j)], preferred_element_type=F32)
-        for half in range(2):
-            part = slice(128 * half, 128 * half + 128)
-            tile = 2 * j + half
-            g_s[j, :, part] = forward_tile(
-                p_s[:, part], tile, lambda i: ck[i, 0, tile_lanes(tile)], unit_mask(tile)
+    def up_product(j, slot):
+        p_s[slot] = jnp.dot(xb[...], cu[:, lanes(j)], preferred_element_type=F32)
+
+    def forward(m, carry):
+        for slot in range(2):
+            j = 2 * m + slot
+            up_product(lax.rem(j + 1, FULL), 1 - slot)
+            for half in range(2):
+                part = slice(128 * half, 128 * half + 128)
+                tile = 2 * j + half
+                g = forward_tile(
+                    p_s[slot, :, part],
+                    tile,
+                    lambda i, tile=tile: ck[i, 0, tile_lanes(tile)],
+                    unit_mask(tile),
+                )
+                g_t[slot, :, part] = g
+                g_s[j, :, part] = g
+            acc2[...] += lax.dot_general(
+                g_t[slot], cd[:, lanes(j)], (((1,), (1,)), ((), ())), preferred_element_type=F32
             )
-        acc2[...] += lax.dot_general(
-            g_s[j], cd[:, lanes(j)], (((1,), (1,)), ((), ())), preferred_element_type=F32
-        )
-        return carry
-
-    lax.fori_loop(0, FULL, forward, 0)
+        return carry
+
+    up_product(0, 0)
+    lax.fori_loop(0, FULL // 2, forward, 0)
 
     lax.fori_loop(1, H, wait_row, 0)
     second = row_in[...].astype(F32).reshape(CELLS, C)
@@ -532,23 +543,20 @@
         j = X * y + x
         down_own[j, :C] = jnp.dot(ebt[...], g_s[j], preferred_element_type=F32).astype(BF16)
 
-    order = (2, 3, 1, 0)
-
-    for k in order:
+    def start_down(k):
         x = lax.rem(my_x + k, X)
         down_slab(1 - my_y, x)
         down_over_y(x).start()
 
-    def own_down(x, carry):
-        down_slab(my_y, x)
-        return carry
-
-    lax.fori_loop(0, X, own_down, 0)
+    start_down(2)
 
     def relay_down(x):
+        j = X * my_y + x
         down_over_y(x).wait_recv()
-        down_sum[x] = (
-            down_own[X * my_y + x].astype(F32) + down_y[x].astype(F32)
+        own = jnp.dot(ebt[...], g_s[j], preferred_element_type=F32)
+        down_sum[x, :C] = (own + down_y[x, :C].astype(F32)).astype(BF16)
+        down_sum[x, 352:] = (
+            down_own[j, 352:].astype(F32) + down_y[x, 352:].astype(F32)
         ).astype(BF16)
 
     def split_down():
@@ -604,21 +612,27 @@
         x = lax.rem(my_x + k, X)
         y = (jnp.int32(SIDES) >> t) & 1
         j = X * y + x
-        p_s[...] = jnp.dot(eb[...], cd[:, lanes(j)], preferred_element_type=F32)
+        p_s[0] = jnp.dot(eb[...], cd[:, lanes(j)], preferred_element_type=F32)
         for half in range(2):
             part = slice(128 * half, 128 * half + 128)
             tile = 2 * j + half
-            p_s[:, part] = backward_tile(
-                p_s[:, part], tile, lambda i: ck[i, 0, tile_lanes(tile)]
+            p_s[0, :, part] = backward_tile(
+                p_s[0, :, part], tile, lambda i: ck[i, 0, tile_lanes(tile)]
             )
             up_own[j, 384:416, part] = (kg[...] * taps).astype(BF16)
         up_own[j, :C] = jnp.dot(
-            xt[...], p_s[...].astype(BF16), preferred_element_type=F32
+            xt[...], p_s[0].astype(BF16), preferred_element_type=F32
         ).astype(BF16)
 
         @pl.when(t < 2)
         def _():
             up_half(t).start()
+
+        for when, which in ((0, 3), (1, 1), (2, 0)):
+
+            @pl.when(t == when)
+            def _():
+                start_down(which)
 
         @pl.when((t == 4) | (t == 5))
         def _():
@@ -739,7 +753,7 @@
             pltpu.VMEM((TILES, CELLS, 128), F32),
             pltpu.VMEM((TILES, CELLS, 128), F32),
             pltpu.VMEM((FULL + 1, CELLS, CHUNK), BF16),
-            pltpu.VMEM((CELLS, CHUNK), F32),
+            pltpu.VMEM((2, CELLS, CHUNK), F32),
             pltpu.VMEM((5, H + 4, H, 128), F32),
             pltpu.VMEM((32, 128), F32),
             pltpu.VMEM((n_img, DOWN_ROWS, CHUNK), BF16),
@@ -752,6 +766,7 @@
             pltpu.VMEM((UP_ROWS, CHUNK), BF16),
             pltpu.VMEM((2, HALF, CHUNK), BF16),
             pltpu.VMEM((2, UP_ROWS, CHUNK), BF16),
+            pltpu.VMEM((2, CELLS, CHUNK), BF16),
             pltpu.SemaphoreType.DMA((9,)),
             pltpu.SemaphoreType.DMA((n_cand,)),
             pltpu.SemaphoreType.DMA((n_cand,)),

time: 75.7 us -> 71.6 us (0.946)
  Pallas kernels: 72.8 us -> 68.7 us
    pallas_call x1, Pallas kernels: 70.5 us -> 66.3 us  [body(): pl.pallas_call(functools.partial(kernel, n_cand, n_img), out_shape=(jax.S...]
where the time goes in v5:
time: 71.6 us; the launch traced here: 71.3 us
  Pallas kernels  68.7 us (96%)
  between operations  2.58 us (4%)
    pallas_call x1, Pallas kernels, body(): pl.pallas_call(functools.partial(kernel, n_cand, n_img), out_shape=(jax.S...  66.3 us
    pallas_call x1, Pallas kernels, body(): pl.pallas_call(finish, out_shape=(jax.ShapeDtypeStruct((own, 1, C), F32),...  2.36 us

profile of v5, /device:TPU:1, one launch (start us, length us, event | category | flops | bytes accessed | tf_op | source)
XLA Modules:
  0.0 71.3 jit_solution(1895086367725478599)
XLA Ops:
  2.6 66.3 %step.1 = (f32[384,384]{1,0:T(8,128)}, f32[32,384]{1,0:T(8,128)}, f32[384,384]{1,0:T(8,128)}) custom-call(f32[1,8,344]{2,1,0:T(8,128)} %x_ref.1, s32[1]{0:T(128)S(6)} %copy.13.layer_ref, s32[1]{0:T(128)S(6)} %copy.14.expand_ref, s32[1]{0:T(128)S(6)} %copy.15.radius_ref, bf16[2,344,2064]{2,1,0:T(8,128)(2,1)} %tu_hbm.1, f32[25,2,2064]{2,1,0:T(2,128)} %bitcast.5, ...), custom_call_target="tpu_custom_call" | custom-call | tf_op jit(solution)/shard_map/step/pallas_call | solution.py:725
  68.9 2.4 %finish.1 = (f32[258,1,344]{2,1,0:T(1,128)}, f32[25,1,258]{2,1,0:T(1,128)}, f32[258,1,344]{2,1,0:T(1,128)}) custom-call(f32[384,384]{1,0:T(8,128)} %get-tuple-element.9.gu_hbm, f32[32,384]{1,0:T(8,128)} %get-tuple-element.10.gk_hbm, f32[384,384]{1,0:T(8,128)} %get-tuple-element.11.gd_hbm), custom_call_target="tpu_custom_call" | custom-call | tf_op jit(solution)/shard_map/finish/pallas_call | solution.py:800

commit v6 on v5

--- a/solution.py
+++ b/solution.py
@@ -502,6 +502,9 @@
             X * my_y + x,
         )
 
+    def side(h):
+        return lax.rem(1 - my_y + h, 2)
+
     def opposite(h):
         return lax.rem(my_x + 3 - 2 * h, X)
 
@@ -515,7 +518,7 @@
 
     def up_half(h):
         return send(
-            up_own.at[X * h + lax.rem(my_x + 2, X)],
+            up_own.at[X * side(h) + lax.rem(my_x + 2, X)],
             up_relay.at[h],
             (up_sem.at[0, 2, 1 + h], up_sem.at[1, 2, 1 + h]),
             X * my_y + opposite(h),
@@ -610,7 +613,7 @@
     def up_step(t, carry):
         k = (jnp.int32(PLACES) >> (2 * t)) & 3
         x = lax.rem(my_x + k, X)
-        y = (jnp.int32(SIDES) >> t) & 1
+        y = side((jnp.int32(SIDES) >> t) & 1)
         j = X * y + x
         p_s[0] = jnp.dot(eb[...], cd[:, lanes(j)], preferred_element_type=F32)
         for half in range(2):
@@ -644,11 +647,11 @@
         def _():
             up_over_x(y, x, my_x).start()
 
-        @pl.when(t == 3)
+        @pl.when(t == 2)
         def _():
             split_down()
 
-        @pl.when(t == 7)
+        @pl.when(t == 6)
         def _():
             join_down(0)
 

time: 71.6 us -> 71.2 us (level)
  no operation moved by 1% of the time
where the time goes in v6:
time: 71.2 us; the launch traced here: 71 us
  Pallas kernels  68.4 us (96%)
  between operations  2.58 us (4%)
    pallas_call x1, Pallas kernels, body(): pl.pallas_call(functools.partial(kernel, n_cand, n_img), out_shape=(jax.S...  66.1 us
    pallas_call x1, Pallas kernels, body(): pl.pallas_call(finish, out_shape=(jax.ShapeDtypeStruct((own, 1, C), F32),...  2.36 us

profile of v6, /device:TPU:1, one launch (start us, length us, event | category | flops | bytes accessed | tf_op | source)
XLA Modules:
  0.0 71.0 jit_solution(13465666095618330302)
XLA Ops:
  2.6 66.1 %step.1 = (f32[384,384]{1,0:T(8,128)}, f32[32,384]{1,0:T(8,128)}, f32[384,384]{1,0:T(8,128)}) custom-call(f32[1,8,344]{2,1,0:T(8,128)} %x_ref.1, s32[1]{0:T(128)S(6)} %copy.13.layer_ref, s32[1]{0:T(128)S(6)} %copy.14.expand_ref, s32[1]{0:T(128)S(6)} %copy.15.radius_ref, bf16[2,344,2064]{2,1,0:T(8,128)(2,1)} %tu_hbm.1, f32[25,2,2064]{2,1,0:T(2,128)} %bitcast.5, ...), custom_call_target="tpu_custom_call" | custom-call | tf_op jit(solution)/shard_map/step/pallas_call | solution.py:728
  68.6 2.4 %finish.1 = (f32[258,1,344]{2,1,0:T(1,128)}, f32[25,1,258]{2,1,0:T(1,128)}, f32[258,1,344]{2,1,0:T(1,128)}) custom-call(f32[384,384]{1,0:T(8,128)} %get-tuple-element.9.gu_hbm, f32[32,384]{1,0:T(8,128)} %get-tuple-element.10.gk_hbm, f32[384,384]{1,0:T(8,128)} %get-tuple-element.11.gd_hbm), custom_call_target="tpu_custom_call" | custom-call | tf_op jit(solution)/shard_map/finish/pallas_call | solution.py:803
